TPU v7x, 256 devices: a whole 4x4x8 slice. The times are simulated.
256 devices in a mesh: ctx: 32 (over x, z), tp: 8 (over y, core).
Axes of the slice: x: 4, y: 4, z: 8, core: 2. Of those that a mesh axis runs over, the one named last changes fastest.
Arguments:
- projected: bfloat16 [4096, 3, 4096], P('ctx', None, 'tp'), may hold values from -6 to 6
- short_filter: float32 [7, 3, 4096], P(None, None, 'tp'), may hold values from -2.4 to 2.4
- long_filter: bfloat16 [256, 2048], P('tp'), may hold values from -0.26516504 to 0.26516504
- out_weight: bfloat16 [4096, 8192], P('tp'), may hold values from -0.09375 to 0.09375
Outputs:
- layer_out: bfloat16 [4096, 8192], P('ctx', 'tp')
All inputs are finite; a program needn't handle non-finite values.
Results may differ from a plain program's by a relative error of at most 0.015.
Values may be sent and summed in bfloat16 or wider, within the bound.
No kernel may reach another device: no remote copies, remote signals or barrier semaphores. Data moves between devices by JAX's collectives and lax.ppermute only.
A program may use at most 64 MiB of HBM per device.

v0:
```python
import math

import jax
import jax.numpy as jnp
from jax import lax
from jax.sharding import PartitionSpec as P


def shifted(array, axis, by):
    size = lax.axis_size(axis)
    pairs = [(i, i + by) for i in range(size) if 0 <= i + by < size]
    return lax.ppermute(array, axis, pairs)


def toeplitz_block(padded_taps, lag_base, count, tok_rows):
    width = tok_rows + count - 1
    groups = padded_taps.shape[0]
    window = lax.dynamic_slice_in_dim(padded_taps, lag_base - (count - 1) + 2 * tok_rows, width, 1)
    flipped = jnp.concatenate([window[:, ::-1], jnp.zeros((groups, 1), window.dtype)], axis=1)
    tiled = jnp.tile(flipped, (1, tok_rows))
    skewed = tiled[:, : tok_rows * width].reshape(groups, tok_rows, width)
    return skewed[:, :, tok_rows - 1 : tok_rows - 1 + count]


def block_term(padded_taps, source, lag_base, tok_rows):
    count, channels = source.shape
    groups = padded_taps.shape[0]
    matrix = toeplitz_block(padded_taps, lag_base, count, tok_rows)
    grouped = source.reshape(count, groups, channels // groups)
    term = jnp.einsum("gts,sgi->tgi", matrix, grouped, preferred_element_type=jnp.float32)
    return term.reshape(tok_rows, channels)


def add_blocks(total, piece, padded_taps, my_start, reach):
    tok_rows = total.shape[0]
    count = piece.shape[0]
    block = math.gcd(count, tok_rows)

    def one_block(index, carry):
        first = index * block
        source = lax.dynamic_slice_in_dim(piece, index * block, block, 0)
        lag_base = my_start - first
        useful = jnp.logical_and(lag_base + tok_rows - 1 >= 0, lag_base - block + 1 <= reach - 1)
        return lax.cond(
            useful,
            lambda running: running + block_term(padded_taps, source, lag_base, tok_rows),
            lambda running: running,
            carry,
        )

    return lax.fori_loop(0, count // block, one_block, total)


def body(projected, short_filter, long_filter, out_weight):
    tok_rows = projected.shape[0]
    taps = short_filter.shape[0]
    groups = long_filter.shape[0]
    reach = long_filter.shape[1]
    my_start = lax.axis_index("ctx") * tok_rows
    border = shifted(projected[tok_rows - (taps - 1) :], "ctx", 1)
    extended = jnp.concatenate([border, projected], axis=0).astype(jnp.float32)
    conved = short_filter[0] * extended[taps - 1 : taps - 1 + tok_rows]
    for offset in range(1, taps):
        conved = (
            conved
            + short_filter[offset] * extended[taps - 1 - offset : taps - 1 - offset + tok_rows]
        )
    values = (conved[:, 1, :] * conved[:, 2, :]).astype(jnp.bfloat16)
    padding = jnp.zeros((groups, 2 * tok_rows), long_filter.dtype)
    padded_taps = jnp.concatenate([padding, long_filter, padding], axis=1)
    empty = jnp.zeros(values.shape, jnp.float32)
    mixed = add_blocks(
        empty, lax.all_gather(values, "ctx", axis=0, tiled=True), padded_taps, my_start, reach
    )
    hidden = (conved[:, 0, :] * mixed).astype(jnp.bfloat16)
    partial_sum = jnp.dot(hidden, out_weight, preferred_element_type=jnp.float32)
    return lax.psum_scatter(partial_sum.astype(jnp.bfloat16), "tp", scatter_dimension=1, tiled=True)


def solution(mesh):
    return jax.shard_map(
        body,
        mesh=mesh,
        in_specs=(P("ctx", None, "tp"), P(None, None, "tp"), P("tp", None), P("tp", None)),
        out_specs=P("ctx", "tp"),
        check_vma=False,
    )
```

profile of v0, /device:TPU:2, one launch (start us, length us, event | category | flops | bytes accessed | tf_op | source)
XLA Modules:
  0.0 382.6 jit_solution(14550529410399828677)
XLA Ops:
  7.5 3.8 collective-permute-start
  13.9 10.5 %collective-permute-done = bf16[6,3,512]{0,2,1:T(8,128)(2,1)S(1)} collective-permute-done((bf16[6,3,512]{0,2,1:T(8,128)(2,1)S(1)}, bf16[6,3,512]{0,2,1:T(8,128)(2,1)S(1)}, u32[]{:S(2)}, u32[]{:S(2)}) %collective-permute-start) | collective-permute-done | bytes 18464 | tf_op jit(solution)/shard_map/ppermute | solution.py:12
  28.5 83.2 %all-gather.3.cloned.1.call-done = bf16[4096,1,512]{0,2,1:T(8,128)(2,1)} async-done(((bf16[128,1,512]{0,2,1:T(8,128)(2,1)}), bf16[4096,1,512]{0,2,1:T(8,128)(2,1)}) %all-gather.3.cloned.1.call-update) | async-done | bytes 4194320 | tf_op jit(solution)/shard_map/all_gather | solution.py:73
  111.7 117.8 %while.20 = (s32[]{:T(128)}, f32[128,512]{0,1:T(8,128)S(1)}, s32[]{:T(128)}, bf16[32,2560]{1,0:T(8,128)(2,1)S(1)}, bf16[4096,512]{0,1:T(8,128)(2,1)}, /*index=5*...) while((s32[]{:T(128)}, f32[128,512]{0,1:T(8,128)S(1)}, s32[]{:T(128)}, ...), condition=%wide.region_3.0_spmd, body=%wide.region_0.0_spmd.sunk | while | flops 16842768 | bytes 17285120 | solution.py:51
  111.8 12.9 %conditional.2 = (f32[128,512]{0,1:T(8,128)S(1)}) conditional(s32[]{:T(128)} %convert_element_type.39, f32[128,512]{0,1:T(8,128)S(1)} %get-tuple-element.299, (s32[]{:T(128)}, bf16[32,2560]{1,0:T(8,128)(2,1)S(1)}, s32[]{:T(128)}, bf16[4096,512]{0,1:T(8,128)(2,1)}, f32[128,512]{0,1:T(8,128)S(1)}) %tuple.78), branch_computations={%region_1.0_spmd, %region_2.0_spmd} | conditional | flops 16842760 | bytes 17284898 | solution.py:44
  114.6 7.8 %reshape.15 = bf16[32,128,255]{2,1,0:T(8,128)(2,1)} reshape(bf16[32,32640]{1,0:T(8,128)(2,1)S(1)} %slice.80) | data formatting | bytes 4177920 | tf_op jit(solution)/shard_map/while/body/eval_jaxpr/cond/branch_1_fun/reshape | solution.py:21
  124.7 12.9 %conditional.2 = (f32[128,512]{0,1:T(8,128)S(1)}) conditional(s32[]{:T(128)} %convert_element_type.39, f32[128,512]{0,1:T(8,128)S(1)} %get-tuple-element.299, (s32[]{:T(128)}, bf16[32,2560]{1,0:T(8,128)(2,1)S(1)}, s32[]{:T(128)}, bf16[4096,512]{0,1:T(8,128)(2,1)}, f32[128,512]{0,1:T(8,128)S(1)}) %tuple.78), branch_computations={%region_1.0_spmd, %region_2.0_spmd} | conditional | flops 16842760 | bytes 17284898 | solution.py:44
  127.5 7.8 %reshape.15 = bf16[32,128,255]{2,1,0:T(8,128)(2,1)} reshape(bf16[32,32640]{1,0:T(8,128)(2,1)S(1)} %slice.80) | data formatting | bytes 4177920 | tf_op jit(solution)/shard_map/while/body/eval_jaxpr/cond/branch_1_fun/reshape | solution.py:21
  137.7 12.9 %conditional.2 = (f32[128,512]{0,1:T(8,128)S(1)}) conditional(s32[]{:T(128)} %convert_element_type.39, f32[128,512]{0,1:T(8,128)S(1)} %get-tuple-element.299, (s32[]{:T(128)}, bf16[32,2560]{1,0:T(8,128)(2,1)S(1)}, s32[]{:T(128)}, bf16[4096,512]{0,1:T(8,128)(2,1)}, f32[128,512]{0,1:T(8,128)S(1)}) %tuple.78), branch_computations={%region_1.0_spmd, %region_2.0_spmd} | conditional | flops 16842760 | bytes 17284898 | solution.py:44
  140.5 7.8 %reshape.15 = bf16[32,128,255]{2,1,0:T(8,128)(2,1)} reshape(bf16[32,32640]{1,0:T(8,128)(2,1)S(1)} %slice.80) | data formatting | bytes 4177920 | tf_op jit(solution)/shard_map/while/body/eval_jaxpr/cond/branch_1_fun/reshape | solution.py:21
  150.7 12.9 %conditional.2 = (f32[128,512]{0,1:T(8,128)S(1)}) conditional(s32[]{:T(128)} %convert_element_type.39, f32[128,512]{0,1:T(8,128)S(1)} %get-tuple-element.299, (s32[]{:T(128)}, bf16[32,2560]{1,0:T(8,128)(2,1)S(1)}, s32[]{:T(128)}, bf16[4096,512]{0,1:T(8,128)(2,1)}, f32[128,512]{0,1:T(8,128)S(1)}) %tuple.78), branch_computations={%region_1.0_spmd, %region_2.0_spmd} | conditional | flops 16842760 | bytes 17284898 | solution.py:44
  153.5 7.8 %reshape.15 = bf16[32,128,255]{2,1,0:T(8,128)(2,1)} reshape(bf16[32,32640]{1,0:T(8,128)(2,1)S(1)} %slice.80) | data formatting | bytes 4177920 | tf_op jit(solution)/shard_map/while/body/eval_jaxpr/cond/branch_1_fun/reshape | solution.py:21
  163.7 12.9 %conditional.2 = (f32[128,512]{0,1:T(8,128)S(1)}) conditional(s32[]{:T(128)} %convert_element_type.39, f32[128,512]{0,1:T(8,128)S(1)} %get-tuple-element.299, (s32[]{:T(128)}, bf16[32,2560]{1,0:T(8,128)(2,1)S(1)}, s32[]{:T(128)}, bf16[4096,512]{0,1:T(8,128)(2,1)}, f32[128,512]{0,1:T(8,128)S(1)}) %tuple.78), branch_computations={%region_1.0_spmd, %region_2.0_spmd} | conditional | flops 16842760 | bytes 17284898 | solution.py:44
  166.5 7.8 %reshape.15 = bf16[32,128,255]{2,1,0:T(8,128)(2,1)} reshape(bf16[32,32640]{1,0:T(8,128)(2,1)S(1)} %slice.80) | data formatting | bytes 4177920 | tf_op jit(solution)/shard_map/while/body/eval_jaxpr/cond/branch_1_fun/reshape | solution.py:21
  176.6 12.9 %conditional.2 = (f32[128,512]{0,1:T(8,128)S(1)}) conditional(s32[]{:T(128)} %convert_element_type.39, f32[128,512]{0,1:T(8,128)S(1)} %get-tuple-element.299, (s32[]{:T(128)}, bf16[32,2560]{1,0:T(8,128)(2,1)S(1)}, s32[]{:T(128)}, bf16[4096,512]{0,1:T(8,128)(2,1)}, f32[128,512]{0,1:T(8,128)S(1)}) %tuple.78), branch_computations={%region_1.0_spmd, %region_2.0_spmd} | conditional | flops 16842760 | bytes 17284898 | solution.py:44
  179.4 7.8 %reshape.15 = bf16[32,128,255]{2,1,0:T(8,128)(2,1)} reshape(bf16[32,32640]{1,0:T(8,128)(2,1)S(1)} %slice.80) | data formatting | bytes 4177920 | tf_op jit(solution)/shard_map/while/body/eval_jaxpr/cond/branch_1_fun/reshape | solution.py:21
  189.6 12.9 %conditional.2 = (f32[128,512]{0,1:T(8,128)S(1)}) conditional(s32[]{:T(128)} %convert_element_type.39, f32[128,512]{0,1:T(8,128)S(1)} %get-tuple-element.299, (s32[]{:T(128)}, bf16[32,2560]{1,0:T(8,128)(2,1)S(1)}, s32[]{:T(128)}, bf16[4096,512]{0,1:T(8,128)(2,1)}, f32[128,512]{0,1:T(8,128)S(1)}) %tuple.78), branch_computations={%region_1.0_spmd, %region_2.0_spmd} | conditional | flops 16842760 | bytes 17284898 | solution.py:44
  192.4 7.8 %reshape.15 = bf16[32,128,255]{2,1,0:T(8,128)(2,1)} reshape(bf16[32,32640]{1,0:T(8,128)(2,1)S(1)} %slice.80) | data formatting | bytes 4177920 | tf_op jit(solution)/shard_map/while/body/eval_jaxpr/cond/branch_1_fun/reshape | solution.py:21
  202.6 12.9 %conditional.2 = (f32[128,512]{0,1:T(8,128)S(1)}) conditional(s32[]{:T(128)} %convert_element_type.39, f32[128,512]{0,1:T(8,128)S(1)} %get-tuple-element.299, (s32[]{:T(128)}, bf16[32,2560]{1,0:T(8,128)(2,1)S(1)}, s32[]{:T(128)}, bf16[4096,512]{0,1:T(8,128)(2,1)}, f32[128,512]{0,1:T(8,128)S(1)}) %tuple.78), branch_computations={%region_1.0_spmd, %region_2.0_spmd} | conditional | flops 16842760 | bytes 17284898 | solution.py:44
  205.4 7.8 %reshape.15 = bf16[32,128,255]{2,1,0:T(8,128)(2,1)} reshape(bf16[32,32640]{1,0:T(8,128)(2,1)S(1)} %slice.80) | data formatting | bytes 4177920 | tf_op jit(solution)/shard_map/while/body/eval_jaxpr/cond/branch_1_fun/reshape | solution.py:21
  215.6 12.9 %conditional.2 = (f32[128,512]{0,1:T(8,128)S(1)}) conditional(s32[]{:T(128)} %convert_element_type.39, f32[128,512]{0,1:T(8,128)S(1)} %get-tuple-element.299, (s32[]{:T(128)}, bf16[32,2560]{1,0:T(8,128)(2,1)S(1)}, s32[]{:T(128)}, bf16[4096,512]{0,1:T(8,128)(2,1)}, f32[128,512]{0,1:T(8,128)S(1)}) %tuple.78), branch_computations={%region_1.0_spmd, %region_2.0_spmd} | conditional | flops 16842760 | bytes 17284898 | solution.py:44
  218.4 7.8 %reshape.15 = bf16[32,128,255]{2,1,0:T(8,128)(2,1)} reshape(bf16[32,32640]{1,0:T(8,128)(2,1)S(1)} %slice.80) | data formatting | bytes 4177920 | tf_op jit(solution)/shard_map/while/body/eval_jaxpr/cond/branch_1_fun/reshape | solution.py:21
  229.5 6.0 %convolution_convert_fusion = bf16[128,8192]{1,0:T(8,128)(2,1)} fusion(bf16[512,8192]{1,0:T(8,128)(2,1)} %param.11, f32[128,512]{0,1:T(8,128)S(1)} %get-tuple-element.232, f32[128,3,512]{0,2,1:T(8,128)S(1)} %fusion.2), kind=kOutput, calls=%fused_computation.5 | convolution fusion | flops 1074921472 | bytes 11010048 | tf_op jit(solution)/shard_map/dot_general | solution.py:76
  235.6 140.2 %reduce-scatter.2.cloned.1.call-done = bf16[128,1024]{1,0:T(8,128)(2,1)} async-done(((bf16[128,8192]{1,0:T(8,128)(2,1)}), bf16[128,1024]{1,0:T(8,128)(2,1)}) %reduce-scatter.2.cloned.1.call-update) | async-done | bytes 262160 | tf_op jit(solution)/shard_map/reduce_scatter | solution.py:77
  (133 shorter events, 53.8 us)
Async XLA Ops:
  6.5 105.2 %all-gather.3.cloned.1.call-start = ((), (), s32[]{:S(2)}) async-start(), calls=%async_computation.2 | async-start | bytes 4325376 | tf_op jit(solution)/shard_map/all_gather | solution.py:73
  7.5 16.8 %collective-permute-start = (bf16[6,3,512]{0,2,1:T(8,128)(2,1)S(1)}, bf16[6,3,512]{0,2,1:T(8,128)(2,1)S(1)}, u32[]{:S(2)}, u32[]{:S(2)}) collective-permute-start(bf16[6,3,512]{0,2,1:T(8,128)(2,1)S(1)} %copy.7), channel_id=1, source_target_pairs={{0,8},{8,16},{16,24},{24,32},{32,40},{40,48},{48,56},{56,64},{64,7... | collective-permute-start | bytes 55304 | tf_op jit(solution)/shard_map/ppermute | solution.py:12
  24.7 3.8 copy-start
  28.4 347.4 %reduce-scatter.2.cloned.1.call-start = ((), (), s32[]{:S(2)}) async-start(), calls=%async_computation.1 | async-start | bytes 2359296 | tf_op jit(solution)/shard_map/reduce_scatter | solution.py:77
Sparse Core Ops, SparseCore 0:
  28.5 83.1 all-gather.2
  235.7 140.0 reduce-scatter.1
where the time goes:
time: 384 us; the launch traced here: 383 us
  waiting for transfers between devices  234 us (61%)
  local copies, waits for them, and re-layouts  98.2 us (26%)
  matrix products  26.7 us (7%)
  between operations  13.5 us (4%)
  other arithmetic  4.52 us (1%)
  starting transfers between devices  3.87 us (1%)
    reduce_scatter x1, waiting for transfers between devices, body(): lax.psum_scatter(partial_sum.astype(jnp.bfloat16), 'tp', scatter_dimensio...  140 us
    all_gather x1, waiting for transfers between devices, body(): lax.all_gather(values, 'ctx', axis=0, tiled=True)  83.2 us
    reshape x9, local copies, waits for them, and re-layouts, toeplitz_block(): skewed = tiled[:, :tok_rows * width].reshape(groups, tok_rows, width)  70 us
    dot_general x9, matrix products, block_term(): jnp.einsum('gts,sgi->tgi', matrix, grouped, preferred_element_type=jnp.fl...  20.7 us
    cond x27, local copies, waits for them, and re-layouts  13.1 us
    ppermute x1, waiting for transfers between devices, shifted(): return lax.ppermute(array, axis, pairs)  10.5 us
    dynamic_slice x9, local copies, waits for them, and re-layouts, one_block(): source = lax.dynamic_slice_in_dim(piece, index * block, block, 0)  8.29 us
  transfers between devices with their start and end apart: 3, of which 3 were waited for; matrix products, arithmetic and copies ran while one was open for 1% of the time, Pallas kernels for 0%

commit v1 on v0

v1 whole, which is shorter than its diff:
```python
import functools

import jax
import jax.numpy as jnp
from jax import lax
from jax.experimental import pallas as pl
from jax.experimental.pallas import tpu as pltpu
from jax.sharding import PartitionSpec as P

BF = jnp.bfloat16
F32 = jnp.float32
VMEM = pl.BlockSpec(memory_space=pltpu.VMEM)
HBM = pl.BlockSpec(memory_space=pltpu.HBM)

EDGE = 8
CHUNKS = 2


def in_hbm(x):
    return pltpu.with_memory_space_constraint(x, pltpu.HBM)


def shaped(shape, dtype=BF):
    return jax.ShapeDtypeStruct(shape, dtype)


def call(kernel, out_shape, in_specs, scratch=(), limit=16, flops=0, nbytes=0):
    many = isinstance(out_shape, (list, tuple))
    return pl.pallas_call(
        kernel,
        out_shape=out_shape,
        in_specs=in_specs,
        out_specs=[VMEM] * len(out_shape) if many else VMEM,
        scratch_shapes=list(scratch),
        compiler_params=pltpu.CompilerParams(vmem_limit_bytes=limit << 20),
        cost_estimate=pl.CostEstimate(flops=flops, bytes_accessed=nbytes, transcendentals=0),
    )


def short_conv(x, sf_ref, feature, lanes):
    total = sf_ref[feature, 0:1, lanes] * x
    for d in range(1, sf_ref.shape[1]):
        total = total + sf_ref[feature, d : d + 1, lanes] * pltpu.roll(x, d, 0)
    return total


def pack_kernel(x_hbm, sf_hbm, out_ref, x_ref, sf_ref, sems, *, gsize):
    feats, tokens, channels = x_hbm.shape
    copies = [pltpu.make_async_copy(sf_hbm, sf_ref, sems.at[feats])]
    copies += [pltpu.make_async_copy(x_hbm.at[f], x_ref.at[f], sems.at[f]) for f in range(feats)]
    for copy in copies:
        copy.start()
    for copy in copies:
        copy.wait()
    pad = jnp.zeros((64 - 2 * EDGE * feats, 128), F32)
    left = lax.broadcasted_iota(jnp.int32, (128 // gsize, 8, 128), 2) < 64
    for j in range(0, channels, 128):
        lanes = slice(j, j + 128)
        groups = slice(j // gsize, (j + 128) // gsize)
        x = [x_ref[f, :, lanes].astype(F32) for f in range(feats)]
        values = short_conv(x[1], sf_ref, 1, lanes) * short_conv(x[2], sf_ref, 2, lanes)
        out_ref[groups, :gsize, :] = values.T.astype(BF).reshape(128 // gsize, gsize, tokens)
        edges = []
        for f in range(feats):
            edges += [x[f][tokens - EDGE :], x[f][:EDGE]]
        edges = jnp.concatenate((edges + [pad]) * 2, axis=0).T.reshape(128 // gsize, gsize, 128)
        out_ref[groups, gsize:, :] = jnp.where(left, edges[:, :8], edges[:, 8:]).astype(BF)


def prep_kernel(x_hbm, sf_hbm, lf_hbm, g_ref, gate_ref, coef_ref, x_ref, sf_ref, lf_ref, sems, *, gsize):
    tok, channels = x_ref.shape
    _, taps, _ = sf_ref.shape
    groups, reach = lf_ref.shape
    lags = reach // tok + 1
    copies = [
        pltpu.make_async_copy(sf_hbm, sf_ref, sems.at[0]),
        pltpu.make_async_copy(lf_hbm, lf_ref, sems.at[1]),
        pltpu.make_async_copy(x_hbm.at[0], x_ref, sems.at[2]),
    ]
    for copy in copies:
        copy.start()
    me = lax.axis_index("ctx")
    for copy in copies:
        copy.wait()
    row = lax.broadcasted_iota(jnp.int32, (8, channels), 0)
    col = lax.broadcasted_iota(jnp.int32, (8, channels), 1)
    lane = lax.broadcasted_iota(jnp.int32, (8, 128), 1)
    for d in range(taps):
        tile = jnp.zeros((8, 128), F32)
        for h in range(2):
            pick = col == row + (me * gsize + 8 * h)
            for f in range(3):
                tap = jnp.sum(jnp.where(pick, sf_ref[f, d : d + 1, :], 0.0), axis=1, keepdims=True)
                tile = jnp.where(lane // 16 == 4 * h + f, jnp.broadcast_to(tap, (8, 128)), tile)
        coef_ref[d] = tile
    s_i = lax.broadcasted_iota(jnp.int32, (tok, tok), 0)
    t_i = lax.broadcasted_iota(jnp.int32, (tok, tok), 1)
    upper = t_i >= s_i
    mine = lax.broadcasted_iota(jnp.int32, (groups, tok), 0) == me
    before = jnp.zeros((tok, tok), F32)
    for k in range(lags):
        if k < lags - 1:
            taps_k = lf_ref[:, k * tok : (k + 1) * tok].astype(F32)
            taps_k = jnp.sum(jnp.where(mine, taps_k, 0.0), axis=0, keepdims=True)
            here = pltpu.roll(jnp.broadcast_to(taps_k, (tok, tok)), 0, 1, stride=1, stride_axis=0)
        else:
            here = jnp.zeros((tok, tok), F32)
        g_ref[k * tok : (k + 1) * tok, :] = jnp.where(upper, here, before).astype(BF)
        before = here
    for j in range(0, channels, 128):
        lanes = slice(j, j + 128)
        gate_ref[:, lanes] = short_conv(x_ref[:, lanes].astype(F32), sf_ref, 0, lanes)


def blocks_of(first, own):
    tp = lax.axis_index("tp")
    y = lax.div(tp, 2)
    core = lax.rem(tp, 2)
    if not own:
        core = 1 - core
    near = jnp.bitwise_xor(y, 1)
    far = 3 - y
    even = core == 0
    if first:
        chips = (jnp.where(even, near, far), 3 - near)
    else:
        chips = (y, jnp.where(even, far, near))
    return [chip * 2 + core for chip in chips]


def fetches(w_hbm, w_ref, sems, wanted):
    cols = w_ref.shape[2]
    copies = []
    for slot, block in enumerate(wanted):
        start = pl.multiple_of(block * cols, cols)
        copies.append(pltpu.make_async_copy(w_hbm.at[:, pl.ds(start, cols)], w_ref.at[slot], sems.at[slot]))
    for copy in copies:
        copy.start()
    return copies


def conv_kernel(x_ref, g_ref, coef_ref, w_hbm, out_ref, w_ref, z_ref, sems, *, gsize):
    copies = fetches(w_hbm, w_ref, sems, blocks_of(True, False) + blocks_of(True, True))
    blocks, _, tok = x_ref.shape
    taps = coef_ref.shape[0]
    lags = g_ref.shape[0] // tok
    lane = lax.broadcasted_iota(jnp.int32, (blocks, 8, tok), 2)
    edge = x_ref[:, gsize:, :].astype(F32)
    before = jnp.concatenate([jnp.zeros((1, 8, tok), F32), edge[:-1]], axis=0)
    edge = jnp.where(lane % (2 * EDGE) < EDGE, before, edge).reshape(blocks * 8, tok)
    conved = jnp.zeros((blocks, 8, tok), F32)
    for d in range(taps):
        turned = edge if d == 0 else pltpu.roll(edge, d, 1)
        conved = conved + coef_ref[d][None] * turned.reshape(blocks, 8, tok)
    conved = conved.reshape(blocks * 8, tok)

    def at(first):
        return pltpu.roll(conved, tok - first, 1).reshape(blocks, 8, tok)

    gate = jnp.concatenate([at(EDGE), at(64 + EDGE)], axis=1)
    key = jnp.concatenate([at(3 * EDGE), at(64 + 3 * EDGE)], axis=1)
    value = jnp.concatenate([at(5 * EDGE), at(64 + 5 * EDGE)], axis=1)
    head = lax.broadcasted_iota(jnp.int32, (blocks, gsize, tok), 2) < EDGE
    values = jnp.where(head, key * value, x_ref[:, :gsize, :].astype(F32))
    values = values.astype(BF).reshape(blocks * gsize, tok)
    for k in range(lags):
        if k:
            z_ref[0 : k * gsize, k * tok : (k + 1) * tok] = jnp.zeros((k * gsize, tok), BF)
        z_ref[k * gsize :, k * tok : (k + 1) * tok] = values[: (blocks - k) * gsize]
    mixed = jnp.dot(z_ref[...], g_ref[...], preferred_element_type=F32).reshape(blocks, gsize, tok)
    out_ref[...] = jnp.where(head, gate * mixed, mixed).astype(BF)
    for copy in copies:
        copy.wait()


def product(ht, weight):
    return jnp.dot(ht, weight, preferred_element_type=F32).astype(BF)


def first_theirs_kernel(h_ref, gate_ref, w_ref, out_ref, ht_ref):
    mixed = h_ref[...].T
    ht_ref[...] = (gate_ref[...] * mixed.astype(F32)).astype(BF)
    ht_ref[:EDGE, :] = mixed[:EDGE]
    for slot in range(2):
        out_ref[slot] = product(ht_ref[...], w_ref[slot])


def first_own_kernel(ht_ref, w_ref, out_ref):
    for slot in range(2):
        out_ref[slot] = product(ht_ref[...], w_ref[slot + 2])


def last_kernel(ht_ref, w_hbm, out_ref, w_ref, sems, *, own):
    copies = fetches(w_hbm, w_ref, sems, blocks_of(False, own))
    for slot in range(2):
        copies[slot].wait()
        out_ref[slot] = product(ht_ref[...], w_ref[slot])


def join_kernel(got_ref, own_ref, ht_in_ref, *refs):
    *out_refs, ht_ref = refs
    ht_ref[...] = ht_in_ref[...]
    width = out_refs[0].shape[2]
    for i, out_ref in enumerate(out_refs):
        lanes = slice(i * width, (i + 1) * width)
        out_ref[...] = (got_ref[:, :, lanes].astype(F32) + own_ref[:, :, lanes].astype(F32)).astype(BF)


def pass_kernel(got_ref, own_ref, in_ref, *refs, chunk):
    out_ref, kept_ref = refs[-2:]
    width = in_ref.shape[2]
    lanes = slice(chunk * width, (chunk + 1) * width)
    total = got_ref[:, :, lanes].astype(F32) + own_ref[:, :, lanes].astype(F32) + in_ref[...].astype(F32)
    kept_ref[...] = total[0]
    out_ref[...] = total[1].astype(BF)


def finish_kernel(*refs):
    *in_refs, out_ref = refs
    count = len(in_refs) // 2
    width = in_refs[0].shape[1]
    for i in range(count):
        out_ref[:, i * width : (i + 1) * width] = (in_refs[i][...] + in_refs[count + i][...].astype(F32)).astype(BF)


def body(projected, short_filter, long_filter, out_weight):
    tok, feats, channels = projected.shape
    groups, reach = long_filter.shape
    gsize = channels // groups
    taps = short_filter.shape[0]
    dout = out_weight.shape[1]
    n_tp = lax.axis_size("tp")
    cols = dout // n_tp
    blocks = lax.axis_size("ctx")
    lags = reach // tok + 1

    x = in_hbm(projected.transpose(1, 0, 2))
    sf = in_hbm(short_filter.transpose(1, 0, 2))
    packed = call(
        functools.partial(pack_kernel, gsize=gsize),
        shaped((groups, gsize + 8, tok)),
        [HBM] * 2,
        scratch=(
            pltpu.VMEM((feats, tok, channels), BF),
            pltpu.VMEM((feats, taps, channels), F32),
            pltpu.SemaphoreType.DMA((feats + 1,)),
        ),
    )(x, sf)
    spread = lax.all_to_all(packed, "ctx", 0, 0, tiled=True)
    toeplitz, gate, coef = call(
        functools.partial(prep_kernel, gsize=gsize),
        [
            shaped((lags * tok, tok)),
            shaped((tok, channels), F32),
            shaped((taps, 8, 128), F32),
        ],
        [HBM] * 3,
        scratch=(
            pltpu.VMEM((tok, channels), BF),
            pltpu.VMEM((feats, taps, channels), F32),
            pltpu.VMEM(long_filter.shape, BF),
            pltpu.SemaphoreType.DMA((3,)),
        ),
    )(x, sf, in_hbm(long_filter))
    weight = in_hbm(out_weight)
    mixed, first_weight = call(
        functools.partial(conv_kernel, gsize=gsize),
        [shaped((blocks, gsize, tok)), shaped((4, channels, cols))],
        [VMEM] * 3 + [HBM],
        scratch=(pltpu.VMEM((blocks * gsize, lags * tok), BF), pltpu.SemaphoreType.DMA((4,))),
    )(spread, toeplitz, coef, weight)
    mixed = lax.all_to_all(mixed, "ctx", 0, 0, tiled=True).reshape(channels, tok)

    def project_last(ht, own):
        return call(
            functools.partial(last_kernel, own=own),
            shaped((2, tok, cols)),
            [VMEM, HBM],
            scratch=(pltpu.VMEM((2, channels, cols), BF), pltpu.SemaphoreType.DMA((2,))),
            flops=4 * tok * channels * cols,
            nbytes=4 * channels * cols,
        )(ht, weight)

    def swap(x, peer):
        return lax.ppermute(x, "tp", [(i, peer(i)) for i in range(n_tp)])

    def partner(i):
        return i ^ 1

    def hop_one(i):
        return i ^ 2 if i % 2 == 0 else 8 - i

    def hop_two(i):
        return 6 - i if i % 2 == 0 else i ^ 2

    width = cols // CHUNKS
    theirs, ht = call(
        first_theirs_kernel, [shaped((2, tok, cols)), shaped((tok, channels))], [VMEM] * 3
    )(mixed, gate, first_weight)
    got = swap(theirs, partner)
    own = call(first_own_kernel, shaped((2, tok, cols)), [VMEM] * 2)(ht, first_weight)
    *sends, ht = call(
        join_kernel, [shaped((2, tok, width))] * CHUNKS + [shaped((tok, channels))], [VMEM] * 3
    )(got, own, ht)
    arrived = []
    for i in range(CHUNKS):
        arrived.append(swap(sends[i], hop_one))
    theirs = project_last(ht, False)
    got = swap(theirs, partner)
    own = project_last(ht, True)
    kept, last = [], []
    for i in range(CHUNKS):
        onward, keep = call(
            functools.partial(pass_kernel, chunk=i),
            [shaped((tok, width)), shaped((tok, width), F32)],
            [VMEM] * (3 + min(i, 1)),
        )(got, own, arrived[i], *kept[-1:])
        kept.append(keep)
        last.append(swap(onward, hop_two))
    return call(finish_kernel, shaped((tok, cols)), [VMEM] * (2 * CHUNKS))(*kept, *last)


def solution(mesh):
    return jax.shard_map(
        body,
        mesh=mesh,
        in_specs=(P("ctx", None, "tp"), P(None, None, "tp"), P("tp", None), P("tp", None)),
        out_specs=P("ctx", "tp"),
        check_vma=False,
    )
```

time: 384 us -> 65.9 us (0.17)
  waiting for transfers between devices: 234 us -> 21.2 us
  local copies, waits for them, and re-layouts: 98.2 us -> 0 us
  matrix products: 26.7 us -> 0 us
  blocking collectives: 0 us -> 14.4 us
  starting transfers between devices: 3.87 us -> 17.3 us
  between operations: 13.5 us -> 0.09 us
  Pallas kernels: 0 us -> 12.6 us
  other arithmetic: 4.52 us -> 0 us
    reduce_scatter x1 -> x0, waiting for transfers between devices: 140 us -> none  [body(): lax.psum_scatter(partial_sum.astype(jnp.bfloat16), 'tp', scatter_dimensio...]
    all_gather x1 -> x0, waiting for transfers between devices: 83.2 us -> none  [body(): lax.all_gather(values, 'ctx', axis=0, tiled=True)]
    reshape x9 -> x0, local copies, waits for them, and re-layouts: 70 us -> none  [toeplitz_block(): skewed = tiled[:, :tok_rows * width].reshape(groups, tok_rows, width)]
    dot_general x10 -> x0, matrix products: 26.7 us -> none  [the longest x9 20.7 us: block_term(): jnp.einsum('gts,sgi->tgi', matrix, grouped, preferred_element_type=jnp.fl...]
    all_to_all x0 -> x1, blocking collectives: none -> 14.4 us  [body(): lax.all_to_all(mixed, 'ctx', 0, 0, tiled=True).reshape(channels, tok)]
    cond x27 -> x0, local copies, waits for them, and re-layouts: 13.1 us -> none
    pallas_call x0 -> x11, Pallas kernels: none -> 12.6 us  [the longest x2 3.77 us: project_last(): call(functools.partial(last_kernel, own=own), shaped((2, tok, cols)), [VM...]
    all_to_all x0 -> x1, starting transfers between devices: none -> 11.6 us  [body(): spread = lax.all_to_all(packed, 'ctx', 0, 0, tiled=True)]
  transfers between devices with their start and end apart: 3 -> 7, of which waited for: 3 -> 6; matrix products, arithmetic and copies ran while one was open for 1% -> 0% of each run, Pallas kernels for 0% -> 6%
where the time goes in v1:
time: 65.9 us; the launch traced here: 65.5 us
  waiting for transfers between devices  21.2 us (32%)
  starting transfers between devices  17.3 us (26%)
  blocking collectives  14.4 us (22%)
  Pallas kernels  12.6 us (19%)
    all_to_all x1, blocking collectives, body(): lax.all_to_all(mixed, 'ctx', 0, 0, tiled=True).reshape(channels, tok)  14.4 us
    ppermute x6, waiting for transfers between devices, swap(): return lax.ppermute(x, 'tp', [(i, peer(i)) for i in range(n_tp)])  12.6 us
    all_to_all x1, starting transfers between devices, body(): spread = lax.all_to_all(packed, 'ctx', 0, 0, tiled=True)  11.6 us
    all_to_all x1, waiting for transfers between devices, body(): spread = lax.all_to_all(packed, 'ctx', 0, 0, tiled=True)  8.6 us
    ppermute x6, starting transfers between devices, swap(): return lax.ppermute(x, 'tp', [(i, peer(i)) for i in range(n_tp)])  5.66 us
    pallas_call x2, Pallas kernels, project_last(): call(functools.partial(last_kernel, own=own), shaped((2, tok, cols)), [VM...  3.77 us
    pallas_call x1, Pallas kernels, body(): call(functools.partial(conv_kernel, gsize=gsize), [shaped((blocks, gsize,...  2.99 us
    pallas_call x1, Pallas kernels, body(): call(functools.partial(pack_kernel, gsize=gsize), shaped((groups, gsize +...  2.35 us
  transfers between devices with their start and end apart: 7, of which 6 were waited for; matrix products, arithmetic and copies ran while one was open for 0% of the time, Pallas kernels for 6%

profile of v1, /device:TPU:2, one launch (start us, length us, event | category | flops | bytes accessed | tf_op | source)
XLA Modules:
  0.0 65.5 jit_solution(13535186428914884267)
XLA Ops:
  0.0 2.3 %shard_map.46 = bf16[32,24,128]{2,1,0:T(8,128)(2,1)} custom-call(bf16[3,128,512]{2,1,0:T(8,128)(2,1)} %bitcast.4, f32[3,7,512]{2,1,0:T(8,128)} %bitcast.6), custom_call_target="tpu_custom_call" | custom-call | tf_op jit(solution)/shard_map/pallas_call | solution.py:239
  2.4 11.6 %all-to-all-start = ((bf16[32,24,128]{2,1,0:T(8,128)(2,1)}), bf16[32,24,128]{2,1,0:T(8,128)(2,1)S(1)}, u32[]{:S(2)}, u32[]{:S(2)}) async-start(bf16[32,24,128]{2,1,0:T(8,128)(2,1)} %shard_map.46), calls=%async_computation | async-start | bytes 393216 | tf_op jit(solution)/shard_map/all_to_all | solution.py:249
  14.0 1.5 %shard_map.47 = (bf16[2176,128]{1,0:T(8,128)(2,1)S(1)}, f32[128,512]{1,0:T(8,128)S(1)}, f32[7,8,128]{2,1,0:T(8,128)S(1)}) custom-call(bf16[3,128,512]{2,1,0:T(8,128)(2,1)} %bitcast.5, f32[3,7,512]{2,1,0:T(8,128)} %bitcast.7, bf16[32,2048]{1,0:T(8,128)(2,1)} %lf_hbm.1), custom_call_target="tpu_custom_call" | custom-call | tf_op jit(solution)/shard_map/pallas_call | solution.py:250
  15.5 8.6 %all-to-all-done.x_ref = bf16[32,24,128]{2,1,0:T(8,128)(2,1)S(1)} async-done(((bf16[32,24,128]{2,1,0:T(8,128)(2,1)}), bf16[32,24,128]{2,1,0:T(8,128)(2,1)S(1)}, u32[]{:S(2)}, u32[]{:S(2)}) %all-to-all-start) | async-done | bytes 196640 | tf_op jit(solution)/shard_map/all_to_all | solution.py:249
  24.1 3.0 %shard_map.48 = (bf16[32,16,128]{2,1,0:T(8,128)(2,1)S(1)}, bf16[4,512,1024]{2,1,0:T(8,128)(2,1)S(1)}) custom-call(bf16[32,24,128]{2,1,0:T(8,128)(2,1)S(1)} %all-to-all-done.x_ref, bf16[2176,128]{1,0:T(8,128)(2,1)S(1)} %get-tuple-element.19.g_ref, f32[7,8,128]{2,1,0:T(8,128)S(1)} %get-tuple-element.20.coef_ref, bf16[512,8192]{1,0:T(8,128)(2,1)} %w_hbm.5), custom_call_target="tpu_custom_call" | custom-call | tf_op jit(solution)/shard_map/pallas_call | solution.py:266
  27.1 14.4 %all_to_all.10 = bf16[32,16,128]{2,1,0:T(8,128)(2,1)S(1)} all-to-all(bf16[32,16,128]{2,1,0:T(8,128)(2,1)S(1)} %get-tuple-element.21), channel_id=1, replica_groups=mesh['ctx'=32,'tp'=8] {'ctx'}, dimensions={0} | all-to-all | bytes 262144 | tf_op jit(solution)/shard_map/all_to_all | solution.py:272
  41.5 0.5 shard_map.49
  42.0 0.1 collective-permute-start
  42.1 0.5 shard_map.50.own_ref
  42.5 1.4 %collective-permute-done.got_ref = bf16[2,128,1024]{2,1,0:T(8,128)(2,1)S(1)} collective-permute-done((bf16[2,128,1024]{2,1,0:T(8,128)(2,1)S(1)}, bf16[2,128,1024]{2,1,0:T(8,128)(2,1)S(1)}, u32[]{:S(2)}, u32[]{:S(2)}) %collective-permute-start) | collective-permute-done | bytes 524320 | tf_op jit(solution)/shard_map/ppermute | solution.py:285
  44.0 0.1 shard_map.51
  44.1 1.9 %shard_map.52 = bf16[2,128,1024]{2,1,0:T(8,128)(2,1)S(1)} custom-call(bf16[128,512]{1,0:T(8,128)(2,1)S(1)} %get-tuple-element.26.ht_ref, bf16[512,8192]{1,0:T(8,128)(2,1)} %w_hbm.5), custom_call_target="tpu_custom_call" | custom-call | flops 268435456 | bytes 2097152 | tf_op jit(solution)/shard_map/pallas_call | solution.py:275
  46.0 0.2 collective-permute-start.1
  46.2 1.6 %collective-permute-start.2 = (bf16[2,128,512]{2,1,0:T(8,128)(2,1)S(1)}, bf16[2,128,512]{2,1,0:T(8,128)(2,1)S(1)}, u32[]{:S(2)}, u32[]{:S(2)}) collective-permute-start(bf16[2,128,512]{2,1,0:T(8,128)(2,1)S(1)} %get-tuple-element.27), channel_id=1, source_target_pairs={{0,2},{1,7},{2,0},{3,5},{4,6},{5,3},{6,4},{7,1},{8,10},{9,15},{10,... | collective-permute-start | bytes 786440 | tf_op jit(solution)/shard_map/ppermute | solution.py:285
  47.8 0.4 collective-permute-start.3
  48.3 1.9 %shard_map.53.own_ref = bf16[2,128,1024]{2,1,0:T(8,128)(2,1)S(1)} custom-call(bf16[128,512]{1,0:T(8,128)(2,1)S(1)} %get-tuple-element.26.ht_ref, bf16[512,8192]{1,0:T(8,128)(2,1)} %w_hbm.5), custom_call_target="tpu_custom_call" | custom-call | flops 268435456 | bytes 2097152 | tf_op jit(solution)/shard_map/pallas_call | solution.py:275
  50.1 2.5 %collective-permute-done.2.in_ref = bf16[2,128,512]{2,1,0:T(8,128)(2,1)S(1)} collective-permute-done((bf16[2,128,512]{2,1,0:T(8,128)(2,1)S(1)}, bf16[2,128,512]{2,1,0:T(8,128)(2,1)S(1)}, u32[]{:S(2)}, u32[]{:S(2)}) %collective-permute-start.2) | collective-permute-done | bytes 262176 | tf_op jit(solution)/shard_map/ppermute | solution.py:285
  52.7 2.7 %collective-permute-done.3.in_ref = bf16[2,128,512]{2,1,0:T(8,128)(2,1)S(1)} collective-permute-done((bf16[2,128,512]{2,1,0:T(8,128)(2,1)S(1)}, bf16[2,128,512]{2,1,0:T(8,128)(2,1)S(1)}, u32[]{:S(2)}, u32[]{:S(2)}) %collective-permute-start.3) | collective-permute-done | bytes 262176 | tf_op jit(solution)/shard_map/ppermute | solution.py:285
  55.4 0.1 shard_map.55
  55.5 3.1 %collective-permute-start.5 = (bf16[128,512]{1,0:T(8,128)(2,1)S(1)}, bf16[128,512]{1,0:T(8,128)(2,1)S(1)}, u32[]{:S(2)}, u32[]{:S(2)}) collective-permute-start(bf16[128,512]{1,0:T(8,128)(2,1)S(1)} %get-tuple-element.32), channel_id=1, source_target_pairs={{0,6},{1,3},{2,4},{3,1},{4,2},{5,7},{6,0},{7,5},{8,14},{9,11},{10,... | collective-permute-start | bytes 393224 | tf_op jit(solution)/shard_map/ppermute | solution.py:285
  58.6 0.2 collective-permute-start.4
  58.8 2.9 %collective-permute-done.5.refs_3_ = bf16[128,512]{1,0:T(8,128)(2,1)S(1)} collective-permute-done((bf16[128,512]{1,0:T(8,128)(2,1)S(1)}, bf16[128,512]{1,0:T(8,128)(2,1)S(1)}, u32[]{:S(2)}, u32[]{:S(2)}) %collective-permute-start.5) | collective-permute-done | bytes 131104 | tf_op jit(solution)/shard_map/ppermute | solution.py:285
  61.8 3.0 %collective-permute-done.4.refs_2_ = bf16[128,512]{1,0:T(8,128)(2,1)S(1)} collective-permute-done((bf16[128,512]{1,0:T(8,128)(2,1)S(1)}, bf16[128,512]{1,0:T(8,128)(2,1)S(1)}, u32[]{:S(2)}, u32[]{:S(2)}) %collective-permute-start.4) | collective-permute-done | bytes 131104 | tf_op jit(solution)/shard_map/ppermute | solution.py:285
  64.8 0.7 %shard_map.56 = bf16[128,1024]{1,0:T(8,128)(2,1)} custom-call(f32[128,512]{1,0:T(8,128)S(1)} %get-tuple-element.28.refs_0_, f32[128,512]{1,0:T(8,128)S(1)} %get-tuple-element.30.refs_1_, bf16[128,512]{1,0:T(8,128)(2,1)S(1)} %collective-permute-done.4.refs_2_, bf16[128,512]{1,0:T(8,128)(2,1)S(1)} %collective-permute-done.5.refs_3_), custom_call_target="tpu_custom_call" | custom-call | tf_op jit(solution)/shard_map/pallas_call | solution.py:320
  (2 shorter events, 0.1 us)
Async XLA Ops:
  2.4 21.8 %all-to-all-start = ((bf16[32,24,128]{2,1,0:T(8,128)(2,1)}), bf16[32,24,128]{2,1,0:T(8,128)(2,1)S(1)}, u32[]{:S(2)}, u32[]{:S(2)}) async-start(bf16[32,24,128]{2,1,0:T(8,128)(2,1)} %shard_map.46), calls=%async_computation | async-start | bytes 393216 | tf_op jit(solution)/shard_map/all_to_all | solution.py:249
  42.0 2.0 %collective-permute-start = (bf16[2,128,1024]{2,1,0:T(8,128)(2,1)S(1)}, bf16[2,128,1024]{2,1,0:T(8,128)(2,1)S(1)}, u32[]{:S(2)}, u32[]{:S(2)}) collective-permute-start(bf16[2,128,1024]{2,1,0:T(8,128)(2,1)S(1)} %get-tuple-element.24), channel_id=1, source_target_pairs={{0,1},{1,0},{2,3},{3,2},{4,5},{5,4},{6,7},{7,6},{8,9},{9,8},{10,11... | collective-permute-start | bytes 1572872 | tf_op jit(solution)/shard_map/ppermute | solution.py:285
  46.0 6.6 %collective-permute-start.1 = (bf16[2,128,1024]{2,1,0:T(8,128)(2,1)S(1)}, bf16[2,128,1024]{2,1,0:T(8,128)(2,1)S(1)}, u32[]{:S(2)}, u32[]{:S(2)}) collective-permute-start(bf16[2,128,1024]{2,1,0:T(8,128)(2,1)S(1)} %shard_map.52), channel_id=1, source_target_pairs={{0,1},{1,0},{2,3},{3,2},{4,5},{5,4},{6,7},{7,6},{8,9},{9,8},{10,11... | collective-permute-start | bytes 1572872 | tf_op jit(solution)/shard_map/ppermute | solution.py:285
  46.2 6.4 %collective-permute-start.2 = (bf16[2,128,512]{2,1,0:T(8,128)(2,1)S(1)}, bf16[2,128,512]{2,1,0:T(8,128)(2,1)S(1)}, u32[]{:S(2)}, u32[]{:S(2)}) collective-permute-start(bf16[2,128,512]{2,1,0:T(8,128)(2,1)S(1)} %get-tuple-element.27), channel_id=1, source_target_pairs={{0,2},{1,7},{2,0},{3,5},{4,6},{5,3},{6,4},{7,1},{8,10},{9,15},{10,... | collective-permute-start | bytes 786440 | tf_op jit(solution)/shard_map/ppermute | solution.py:285
  47.8 7.6 %collective-permute-start.3 = (bf16[2,128,512]{2,1,0:T(8,128)(2,1)S(1)}, bf16[2,128,512]{2,1,0:T(8,128)(2,1)S(1)}, u32[]{:S(2)}, u32[]{:S(2)}) collective-permute-start(bf16[2,128,512]{2,1,0:T(8,128)(2,1)S(1)} %get-tuple-element.29), channel_id=1, source_target_pairs={{0,2},{1,7},{2,0},{3,5},{4,6},{5,3},{6,4},{7,1},{8,10},{9,15},{10,... | collective-permute-start | bytes 786440 | tf_op jit(solution)/shard_map/ppermute | solution.py:285
  55.5 6.3 %collective-permute-start.5 = (bf16[128,512]{1,0:T(8,128)(2,1)S(1)}, bf16[128,512]{1,0:T(8,128)(2,1)S(1)}, u32[]{:S(2)}, u32[]{:S(2)}) collective-permute-start(bf16[128,512]{1,0:T(8,128)(2,1)S(1)} %get-tuple-element.32), channel_id=1, source_target_pairs={{0,6},{1,3},{2,4},{3,1},{4,2},{5,7},{6,0},{7,5},{8,14},{9,11},{10,... | collective-permute-start | bytes 393224 | tf_op jit(solution)/shard_map/ppermute | solution.py:285
  58.6 6.2 %collective-permute-start.4 = (bf16[128,512]{1,0:T(8,128)(2,1)S(1)}, bf16[128,512]{1,0:T(8,128)(2,1)S(1)}, u32[]{:S(2)}, u32[]{:S(2)}) collective-permute-start(bf16[128,512]{1,0:T(8,128)(2,1)S(1)} %get-tuple-element.31), channel_id=1, source_target_pairs={{0,6},{1,3},{2,4},{3,1},{4,2},{5,7},{6,0},{7,5},{8,14},{9,11},{10,... | collective-permute-start | bytes 393224 | tf_op jit(solution)/shard_map/ppermute | solution.py:285

commit v2 on v1

--- a/solution.py
+++ b/solution.py
@@ -13,7 +13,8 @@
 HBM = pl.BlockSpec(memory_space=pltpu.HBM)
 
 EDGE = 8
-CHUNKS = 2
+SPLIT = (0, 768, 1024)
+CHUNKS = len(SPLIT) - 1
 
 
 def in_hbm(x):
@@ -24,13 +25,13 @@
     return jax.ShapeDtypeStruct(shape, dtype)
 
 
-def call(kernel, out_shape, in_specs, scratch=(), limit=16, flops=0, nbytes=0):
+def call(kernel, out_shape, in_specs, scratch=(), limit=16, flops=0, nbytes=0, out_specs=None):
     many = isinstance(out_shape, (list, tuple))
     return pl.pallas_call(
         kernel,
         out_shape=out_shape,
         in_specs=in_specs,
-        out_specs=[VMEM] * len(out_shape) if many else VMEM,
+        out_specs=out_specs or ([VMEM] * len(out_shape) if many else VMEM),
         scratch_shapes=list(scratch),
         compiler_params=pltpu.CompilerParams(vmem_limit_bytes=limit << 20),
         cost_estimate=pl.CostEstimate(flops=flops, bytes_accessed=nbytes, transcendentals=0),
@@ -44,27 +45,48 @@
     return total
 
 
-def pack_kernel(x_hbm, sf_hbm, out_ref, x_ref, sf_ref, sems, *, gsize):
+def pack_kernel(x_hbm, sf_hbm, out_hbm, x_ref, head_ref, tail_ref, sf_ref, out_ref, sems, *, gsize):
     feats, tokens, channels = x_hbm.shape
-    copies = [pltpu.make_async_copy(sf_hbm, sf_ref, sems.at[feats])]
-    copies += [pltpu.make_async_copy(x_hbm.at[f], x_ref.at[f], sems.at[f]) for f in range(feats)]
-    for copy in copies:
+    parts = channels // 128
+    few = 128 // gsize
+    firsts = [
+        pltpu.make_async_copy(sf_hbm, sf_ref, sems.at[parts]),
+        pltpu.make_async_copy(x_hbm.at[0, :EDGE], head_ref, sems.at[parts + 1]),
+        pltpu.make_async_copy(x_hbm.at[0, tokens - EDGE :], tail_ref, sems.at[parts + 2]),
+    ]
+    reads = [
+        pltpu.make_async_copy(
+            x_hbm.at[1:, :, j * 128 : (j + 1) * 128], x_ref.at[:, :, j * 128 : (j + 1) * 128], sems.at[j]
+        )
+        for j in range(parts)
+    ]
+    writes = [
+        pltpu.make_async_copy(
+            out_ref.at[j * few : (j + 1) * few], out_hbm.at[j * few : (j + 1) * few], sems.at[parts + 3 + j]
+        )
+        for j in range(parts)
+    ]
+    for copy in firsts + reads:
         copy.start()
-    for copy in copies:
+    for copy in firsts:
         copy.wait()
     pad = jnp.zeros((64 - 2 * EDGE * feats, 128), F32)
-    left = lax.broadcasted_iota(jnp.int32, (128 // gsize, 8, 128), 2) < 64
-    for j in range(0, channels, 128):
-        lanes = slice(j, j + 128)
-        groups = slice(j // gsize, (j + 128) // gsize)
-        x = [x_ref[f, :, lanes].astype(F32) for f in range(feats)]
-        values = short_conv(x[1], sf_ref, 1, lanes) * short_conv(x[2], sf_ref, 2, lanes)
-        out_ref[groups, :gsize, :] = values.T.astype(BF).reshape(128 // gsize, gsize, tokens)
-        edges = []
-        for f in range(feats):
+    left = lax.broadcasted_iota(jnp.int32, (few, 8, 128), 2) < 64
+    for j in range(parts):
+        lanes = slice(j * 128, (j + 1) * 128)
+        groups = slice(j * few, (j + 1) * few)
+        reads[j].wait()
+        x = [x_ref[f, :, lanes].astype(F32) for f in range(feats - 1)]
+        values = short_conv(x[0], sf_ref, 1, lanes) * short_conv(x[1], sf_ref, 2, lanes)
+        out_ref[groups, :gsize, :] = values.T.astype(BF).reshape(few, gsize, tokens)
+        edges = [tail_ref[:, lanes].astype(F32), head_ref[:, lanes].astype(F32)]
+        for f in range(feats - 1):
             edges += [x[f][tokens - EDGE :], x[f][:EDGE]]
-        edges = jnp.concatenate((edges + [pad]) * 2, axis=0).T.reshape(128 // gsize, gsize, 128)
+        edges = jnp.concatenate((edges + [pad]) * 2, axis=0).T.reshape(few, gsize, 128)
         out_ref[groups, gsize:, :] = jnp.where(left, edges[:, :8], edges[:, 8:]).astype(BF)
+        writes[j].start()
+    for copy in writes:
+        copy.wait()
 
 
 def prep_kernel(x_hbm, sf_hbm, lf_hbm, g_ref, gate_ref, coef_ref, x_ref, sf_ref, lf_ref, sems, *, gsize):
@@ -105,8 +127,12 @@
             here = pltpu.roll(jnp.broadcast_to(taps_k, (tok, tok)), 0, 1, stride=1, stride_axis=0)
         else:
             here = jnp.zeros((tok, tok), F32)
-        g_ref[k * tok : (k + 1) * tok, :] = jnp.where(upper, here, before).astype(BF)
+        block = jnp.where(upper, here, before).astype(BF)
+        g_ref[k * tok : (k + 1) * tok, tok:] = block
+        g_ref[(k + 1) * tok : (k + 2) * tok, :tok] = block
         before = here
+    g_ref[:tok, :tok] = jnp.zeros((tok, tok), BF)
+    g_ref[lags * tok :, tok:] = jnp.zeros((tok, tok), BF)
     for j in range(0, channels, 128):
         lanes = slice(j, j + 128)
         gate_ref[:, lanes] = short_conv(x_ref[:, lanes].astype(F32), sf_ref, 0, lanes)
@@ -143,7 +169,6 @@
     copies = fetches(w_hbm, w_ref, sems, blocks_of(True, False) + blocks_of(True, True))
     blocks, _, tok = x_ref.shape
     taps = coef_ref.shape[0]
-    lags = g_ref.shape[0] // tok
     lane = lax.broadcasted_iota(jnp.int32, (blocks, 8, tok), 2)
     edge = x_ref[:, gsize:, :].astype(F32)
     before = jnp.concatenate([jnp.zeros((1, 8, tok), F32), edge[:-1]], axis=0)
@@ -162,12 +187,16 @@
     value = jnp.concatenate([at(5 * EDGE), at(64 + 5 * EDGE)], axis=1)
     head = lax.broadcasted_iota(jnp.int32, (blocks, gsize, tok), 2) < EDGE
     values = jnp.where(head, key * value, x_ref[:, :gsize, :].astype(F32))
-    values = values.astype(BF).reshape(blocks * gsize, tok)
-    for k in range(lags):
-        if k:
-            z_ref[0 : k * gsize, k * tok : (k + 1) * tok] = jnp.zeros((k * gsize, tok), BF)
-        z_ref[k * gsize :, k * tok : (k + 1) * tok] = values[: (blocks - k) * gsize]
-    mixed = jnp.dot(z_ref[...], g_ref[...], preferred_element_type=F32).reshape(blocks, gsize, tok)
+    values = values.astype(BF).reshape(blocks // 2, 2, gsize, tok)
+    rows = blocks // 2 * gsize
+    for k in range(g_ref.shape[0] // tok):
+        source = values[:, 1 - k % 2].reshape(rows, tok)
+        skip = k // 2 * gsize
+        if skip:
+            z_ref[:skip, k * tok : (k + 1) * tok] = jnp.zeros((skip, tok), BF)
+        z_ref[skip:, k * tok : (k + 1) * tok] = source[: rows - skip]
+    mixed = jnp.dot(z_ref[...], g_ref[...], preferred_element_type=F32).reshape(blocks // 2, gsize, 2 * tok)
+    mixed = jnp.stack([mixed[:, :, :tok], mixed[:, :, tok:]], axis=1).reshape(blocks, gsize, tok)
     out_ref[...] = jnp.where(head, gate * mixed, mixed).astype(BF)
     for copy in copies:
         copy.wait()
@@ -185,31 +214,28 @@
         out_ref[slot] = product(ht_ref[...], w_ref[slot])
 
 
-def first_own_kernel(ht_ref, w_ref, out_ref):
+def first_own_kernel(ht_ref, w_ref, w_hbm, out_ref, last_ref, sems):
+    copies = fetches(w_hbm, last_ref, sems, blocks_of(False, False) + blocks_of(False, True))
     for slot in range(2):
         out_ref[slot] = product(ht_ref[...], w_ref[slot + 2])
-
-
-def last_kernel(ht_ref, w_hbm, out_ref, w_ref, sems, *, own):
-    copies = fetches(w_hbm, w_ref, sems, blocks_of(False, own))
+    for copy in copies:
+        copy.wait()
+
+
+def last_kernel(ht_ref, w_ref, out_ref, *, first):
     for slot in range(2):
-        copies[slot].wait()
-        out_ref[slot] = product(ht_ref[...], w_ref[slot])
-
-
-def join_kernel(got_ref, own_ref, ht_in_ref, *refs):
-    *out_refs, ht_ref = refs
+        out_ref[slot] = product(ht_ref[...], w_ref[first + slot])
+
+
+def join_kernel(got_ref, own_ref, ht_in_ref, out_ref, ht_ref, *, chunk):
     ht_ref[...] = ht_in_ref[...]
-    width = out_refs[0].shape[2]
-    for i, out_ref in enumerate(out_refs):
-        lanes = slice(i * width, (i + 1) * width)
-        out_ref[...] = (got_ref[:, :, lanes].astype(F32) + own_ref[:, :, lanes].astype(F32)).astype(BF)
+    lanes = slice(SPLIT[chunk], SPLIT[chunk + 1])
+    out_ref[...] = (got_ref[:, :, lanes].astype(F32) + own_ref[:, :, lanes].astype(F32)).astype(BF)
 
 
 def pass_kernel(got_ref, own_ref, in_ref, *refs, chunk):
     out_ref, kept_ref = refs[-2:]
-    width = in_ref.shape[2]
-    lanes = slice(chunk * width, (chunk + 1) * width)
+    lanes = slice(SPLIT[chunk], SPLIT[chunk + 1])
     total = got_ref[:, :, lanes].astype(F32) + own_ref[:, :, lanes].astype(F32) + in_ref[...].astype(F32)
     kept_ref[...] = total[0]
     out_ref[...] = total[1].astype(BF)
@@ -217,10 +243,9 @@
 
 def finish_kernel(*refs):
     *in_refs, out_ref = refs
-    count = len(in_refs) // 2
-    width = in_refs[0].shape[1]
-    for i in range(count):
-        out_ref[:, i * width : (i + 1) * width] = (in_refs[i][...] + in_refs[count + i][...].astype(F32)).astype(BF)
+    for i in range(CHUNKS):
+        total = in_refs[i][...] + in_refs[CHUNKS + i][...].astype(F32)
+        out_ref[:, SPLIT[i] : SPLIT[i + 1]] = total.astype(BF)
 
 
 def body(projected, short_filter, long_filter, out_weight):
@@ -241,16 +266,20 @@
         shaped((groups, gsize + 8, tok)),
         [HBM] * 2,
         scratch=(
-            pltpu.VMEM((feats, tok, channels), BF),
+            pltpu.VMEM((feats - 1, tok, channels), BF),
+            pltpu.VMEM((EDGE, channels), BF),
+            pltpu.VMEM((EDGE, channels), BF),
             pltpu.VMEM((feats, taps, channels), F32),
-            pltpu.SemaphoreType.DMA((feats + 1,)),
+            pltpu.VMEM((groups, gsize + 8, tok), BF),
+            pltpu.SemaphoreType.DMA((2 * channels // 128 + 3,)),
         ),
+        out_specs=HBM,
     )(x, sf)
     spread = lax.all_to_all(packed, "ctx", 0, 0, tiled=True)
     toeplitz, gate, coef = call(
         functools.partial(prep_kernel, gsize=gsize),
         [
-            shaped((lags * tok, tok)),
+            shaped(((lags + 1) * tok, 2 * tok)),
             shaped((tok, channels), F32),
             shaped((taps, 8, 128), F32),
         ],
@@ -267,19 +296,18 @@
         functools.partial(conv_kernel, gsize=gsize),
         [shaped((blocks, gsize, tok)), shaped((4, channels, cols))],
         [VMEM] * 3 + [HBM],
-        scratch=(pltpu.VMEM((blocks * gsize, lags * tok), BF), pltpu.SemaphoreType.DMA((4,))),
+        scratch=(pltpu.VMEM((blocks // 2 * gsize, (lags + 1) * tok), BF), pltpu.SemaphoreType.DMA((4,))),
     )(spread, toeplitz, coef, weight)
     mixed = lax.all_to_all(mixed, "ctx", 0, 0, tiled=True).reshape(channels, tok)
 
-    def project_last(ht, own):
+    def project_last(ht, first):
         return call(
-            functools.partial(last_kernel, own=own),
+            functools.partial(last_kernel, first=first),
             shaped((2, tok, cols)),
-            [VMEM, HBM],
-            scratch=(pltpu.VMEM((2, channels, cols), BF), pltpu.SemaphoreType.DMA((2,))),
+            [VMEM] * 2,
             flops=4 * tok * channels * cols,
             nbytes=4 * channels * cols,
-        )(ht, weight)
+        )(ht, last_weight)
 
     def swap(x, peer):
         return lax.ppermute(x, "tp", [(i, peer(i)) for i in range(n_tp)])
@@ -293,26 +321,31 @@
     def hop_two(i):
         return 6 - i if i % 2 == 0 else i ^ 2
 
-    width = cols // CHUNKS
+    widths = [SPLIT[i + 1] - SPLIT[i] for i in range(CHUNKS)]
     theirs, ht = call(
         first_theirs_kernel, [shaped((2, tok, cols)), shaped((tok, channels))], [VMEM] * 3
     )(mixed, gate, first_weight)
     got = swap(theirs, partner)
-    own = call(first_own_kernel, shaped((2, tok, cols)), [VMEM] * 2)(ht, first_weight)
-    *sends, ht = call(
-        join_kernel, [shaped((2, tok, width))] * CHUNKS + [shaped((tok, channels))], [VMEM] * 3
-    )(got, own, ht)
+    own, last_weight = call(
+        first_own_kernel,
+        [shaped((2, tok, cols)), shaped((4, channels, cols))],
+        [VMEM] * 2 + [HBM],
+        scratch=(pltpu.SemaphoreType.DMA((4,)),),
+    )(ht, first_weight, weight)
     arrived = []
     for i in range(CHUNKS):
-        arrived.append(swap(sends[i], hop_one))
-    theirs = project_last(ht, False)
+        send, ht = call(
+            functools.partial(join_kernel, chunk=i), [shaped((2, tok, widths[i])), shaped((tok, channels))], [VMEM] * 3
+        )(got, own, ht)
+        arrived.append(swap(send, hop_one))
+    theirs = project_last(ht, 0)
     got = swap(theirs, partner)
-    own = project_last(ht, True)
+    own = project_last(ht, 2)
     kept, last = [], []
     for i in range(CHUNKS):
         onward, keep = call(
             functools.partial(pass_kernel, chunk=i),
-            [shaped((tok, width)), shaped((tok, width), F32)],
+            [shaped((tok, widths[i])), shaped((tok, widths[i]), F32)],
             [VMEM] * (3 + min(i, 1)),
         )(got, own, arrived[i], *kept[-1:])
         kept.append(keep)

time: 65.9 us -> 63.3 us (0.961)
  waiting for transfers between devices: 21.2 us -> 18.2 us
  starting transfers between devices: 17.3 us -> 18.7 us
  Pallas kernels: 12.6 us -> 11.6 us
    ppermute x6, waiting for transfers between devices: 12.6 us -> 9.61 us  [swap(): return lax.ppermute(x, 'tp', [(i, peer(i)) for i in range(n_tp)])]
    ppermute x6, starting transfers between devices: 5.66 us -> 7.05 us  [swap(): return lax.ppermute(x, 'tp', [(i, peer(i)) for i in range(n_tp)])]
    pallas_call x7 -> x8, Pallas kernels: 6.06 us -> 5.3 us  [the longest x1 2.53 us: body(): call(first_own_kernel, [shaped((2, tok, cols)), shaped((4, channels, cols...]
  transfers between devices with their start and end apart: 7 -> 7, of which waited for: 6 -> 3; matrix products, arithmetic and copies ran while one was open for 0% -> 0% of each run, Pallas kernels for 6% -> 7%
where the time goes in v2:
time: 63.3 us; the launch traced here: 63 us
  starting transfers between devices  18.7 us (30%)
  waiting for transfers between devices  18.2 us (29%)
  blocking collectives  14.4 us (23%)
  Pallas kernels  11.6 us (18%)
    all_to_all x1, blocking collectives, body(): lax.all_to_all(mixed, 'ctx', 0, 0, tiled=True).reshape(channels, tok)  14.4 us
    all_to_all x1, starting transfers between devices, body(): spread = lax.all_to_all(packed, 'ctx', 0, 0, tiled=True)  11.6 us
    ppermute x6, waiting for transfers between devices, swap(): return lax.ppermute(x, 'tp', [(i, peer(i)) for i in range(n_tp)])  9.61 us
    all_to_all x1, waiting for transfers between devices, body(): spread = lax.all_to_all(packed, 'ctx', 0, 0, tiled=True)  8.59 us
    ppermute x6, starting transfers between devices, swap(): return lax.ppermute(x, 'tp', [(i, peer(i)) for i in range(n_tp)])  7.05 us
    pallas_call x1, Pallas kernels, body(): call(functools.partial(conv_kernel, gsize=gsize), [shaped((blocks, gsize,...  2.72 us
    pallas_call x1, Pallas kernels, body(): call(first_own_kernel, [shaped((2, tok, cols)), shaped((4, channels, cols...  2.53 us
    pallas_call x1, Pallas kernels, body(): call(functools.partial(pack_kernel, gsize=gsize), shaped((groups, gsize +...  2.38 us
  transfers between devices with their start and end apart: 7, of which 3 were waited for; matrix products, arithmetic and copies ran while one was open for 0% of the time, Pallas kernels for 7%

profile of v2, /device:TPU:2, one launch (start us, length us, event | category | flops | bytes accessed | tf_op | source)
XLA Modules:
  0.0 63.0 jit_solution(17639043329605139580)
XLA Ops:
  0.0 2.4 %shard_map.46 = bf16[32,24,128]{2,1,0:T(8,128)(2,1)} custom-call(bf16[3,128,512]{2,1,0:T(8,128)(2,1)} %bitcast.4, f32[3,7,512]{2,1,0:T(8,128)} %bitcast.6), custom_call_target="tpu_custom_call" | custom-call | tf_op jit(solution)/shard_map/pallas_call | solution.py:264
  2.4 11.6 %all-to-all-start = ((bf16[32,24,128]{2,1,0:T(8,128)(2,1)}), bf16[32,24,128]{2,1,0:T(8,128)(2,1)S(1)}, u32[]{:S(2)}, u32[]{:S(2)}) async-start(bf16[32,24,128]{2,1,0:T(8,128)(2,1)} %shard_map.46), calls=%async_computation | async-start | bytes 393216 | tf_op jit(solution)/shard_map/all_to_all | solution.py:278
  14.0 1.5 %shard_map.47 = (bf16[2304,256]{1,0:T(8,128)(2,1)S(1)}, f32[128,512]{1,0:T(8,128)S(1)}, f32[7,8,128]{2,1,0:T(8,128)S(1)}) custom-call(bf16[3,128,512]{2,1,0:T(8,128)(2,1)} %bitcast.5, f32[3,7,512]{2,1,0:T(8,128)} %bitcast.7, bf16[32,2048]{1,0:T(8,128)(2,1)} %lf_hbm.1), custom_call_target="tpu_custom_call" | custom-call | tf_op jit(solution)/shard_map/pallas_call | solution.py:279
  15.6 8.6 %all-to-all-done.x_ref = bf16[32,24,128]{2,1,0:T(8,128)(2,1)S(1)} async-done(((bf16[32,24,128]{2,1,0:T(8,128)(2,1)}), bf16[32,24,128]{2,1,0:T(8,128)(2,1)S(1)}, u32[]{:S(2)}, u32[]{:S(2)}) %all-to-all-start) | async-done | bytes 196640 | tf_op jit(solution)/shard_map/all_to_all | solution.py:278
  24.2 2.7 %shard_map.48 = (bf16[32,16,128]{2,1,0:T(8,128)(2,1)S(1)}, bf16[4,512,1024]{2,1,0:T(8,128)(2,1)S(1)}) custom-call(bf16[32,24,128]{2,1,0:T(8,128)(2,1)S(1)} %all-to-all-done.x_ref, bf16[2304,256]{1,0:T(8,128)(2,1)S(1)} %get-tuple-element.22.g_ref, f32[7,8,128]{2,1,0:T(8,128)S(1)} %get-tuple-element.23.coef_ref, bf16[512,8192]{1,0:T(8,128)(2,1)} %w_hbm.3), custom_call_target="tpu_custom_call" | custom-call | tf_op jit(solution)/shard_map/pallas_call | solution.py:295
  26.9 14.4 %all_to_all.10 = bf16[32,16,128]{2,1,0:T(8,128)(2,1)S(1)} all-to-all(bf16[32,16,128]{2,1,0:T(8,128)(2,1)S(1)} %get-tuple-element.24), channel_id=1, replica_groups=mesh['ctx'=32,'tp'=8] {'ctx'}, dimensions={0} | all-to-all | bytes 262144 | tf_op jit(solution)/shard_map/all_to_all | solution.py:301
  41.3 0.5 shard_map.49
  41.7 0.1 collective-permute-start
  41.8 2.5 %shard_map.50 = (bf16[2,128,1024]{2,1,0:T(8,128)(2,1)S(1)}, bf16[4,512,1024]{2,1,0:T(8,128)(2,1)S(1)}) custom-call(bf16[128,512]{1,0:T(8,128)(2,1)S(1)} %get-tuple-element.28.ht_ref.ht_in_ref, bf16[4,512,1024]{2,1,0:T(8,128)(2,1)S(1)} %get-tuple-element.26.w_ref, bf16[512,8192]{1,0:T(8,128)(2,1)} %w_hbm.3), custom_call_target="tpu_custom_call" | custom-call | tf_op jit(solution)/shard_map/pallas_call | solution.py:329
  44.4 0.0 collective-permute-done.got_ref
  44.4 0.1 shard_map.51
  44.6 0.4 shard_map.53
  45.0 0.6 collective-permute-start.1
  45.6 1.6 %collective-permute-start.2 = (bf16[2,128,768]{2,1,0:T(8,128)(2,1)S(1)}, bf16[2,128,768]{2,1,0:T(8,128)(2,1)S(1)}, u32[]{:S(2)}, u32[]{:S(2)}) collective-permute-start(bf16[2,128,768]{2,1,0:T(8,128)(2,1)S(1)} %get-tuple-element.33), channel_id=1, source_target_pairs={{0,2},{1,7},{2,0},{3,5},{4,6},{5,3},{6,4},{7,1},{8,10},{9,15},{10,... | collective-permute-start | bytes 1179656 | tf_op jit(solution)/shard_map/ppermute | solution.py:313
  47.2 0.4 collective-permute-start.3
  47.6 0.4 shard_map.54.own_ref
  48.1 5.3 %collective-permute-done.2.in_ref = bf16[2,128,768]{2,1,0:T(8,128)(2,1)S(1)} collective-permute-done((bf16[2,128,768]{2,1,0:T(8,128)(2,1)S(1)}, bf16[2,128,768]{2,1,0:T(8,128)(2,1)S(1)}, u32[]{:S(2)}, u32[]{:S(2)}) %collective-permute-start.2) | collective-permute-done | bytes 393248 | tf_op jit(solution)/shard_map/ppermute | solution.py:313
  53.4 0.0 collective-permute-done.1.got_ref
  53.4 0.1 shard_map.55
  53.5 3.1 %collective-permute-start.4 = (bf16[128,768]{1,0:T(8,128)(2,1)S(1)}, bf16[128,768]{1,0:T(8,128)(2,1)S(1)}, u32[]{:S(2)}, u32[]{:S(2)}) collective-permute-start(bf16[128,768]{1,0:T(8,128)(2,1)S(1)} %get-tuple-element.37), channel_id=1, source_target_pairs={{0,6},{1,3},{2,4},{3,1},{4,2},{5,7},{6,0},{7,5},{8,14},{9,11},{10,... | collective-permute-start | bytes 589832 | tf_op jit(solution)/shard_map/ppermute | solution.py:313
  56.6 0.0 collective-permute-done.3.in_ref
  56.7 1.3 %collective-permute-start.5 = (bf16[128,256]{1,0:T(8,128)(2,1)S(1)}, bf16[128,256]{1,0:T(8,128)(2,1)S(1)}, u32[]{:S(2)}, u32[]{:S(2)}) collective-permute-start(bf16[128,256]{1,0:T(8,128)(2,1)S(1)} %get-tuple-element.38), channel_id=1, source_target_pairs={{0,6},{1,3},{2,4},{3,1},{4,2},{5,7},{6,0},{7,5},{8,14},{9,11},{10,... | collective-permute-start | bytes 196616 | tf_op jit(solution)/shard_map/ppermute | solution.py:313
  57.9 4.3 %collective-permute-done.5.refs_3_ = bf16[128,256]{1,0:T(8,128)(2,1)S(1)} collective-permute-done((bf16[128,256]{1,0:T(8,128)(2,1)S(1)}, bf16[128,256]{1,0:T(8,128)(2,1)S(1)}, u32[]{:S(2)}, u32[]{:S(2)}) %collective-permute-start.5) | collective-permute-done | bytes 65568 | tf_op jit(solution)/shard_map/ppermute | solution.py:313
  62.2 0.7 %shard_map.57 = bf16[128,1024]{1,0:T(8,128)(2,1)} custom-call(f32[128,768]{1,0:T(8,128)S(1)} %get-tuple-element.34.refs_0_, f32[128,256]{1,0:T(8,128)S(1)} %get-tuple-element.36.refs_1_, bf16[128,768]{1,0:T(8,128)(2,1)S(1)} %collective-permute-done.4.refs_2_, bf16[128,256]{1,0:T(8,128)(2,1)S(1)} %collective-permute-done.5.refs_3_), custom_call_target="tpu_custom_call" | custom-call | tf_op jit(solution)/shard_map/pallas_call | solution.py:353
  (3 shorter events, 0.1 us)
Async XLA Ops:
  2.4 21.8 %all-to-all-start = ((bf16[32,24,128]{2,1,0:T(8,128)(2,1)}), bf16[32,24,128]{2,1,0:T(8,128)(2,1)S(1)}, u32[]{:S(2)}, u32[]{:S(2)}) async-start(bf16[32,24,128]{2,1,0:T(8,128)(2,1)} %shard_map.46), calls=%async_computation | async-start | bytes 393216 | tf_op jit(solution)/shard_map/all_to_all | solution.py:278
  41.7 2.6 %collective-permute-start = (bf16[2,128,1024]{2,1,0:T(8,128)(2,1)S(1)}, bf16[2,128,1024]{2,1,0:T(8,128)(2,1)S(1)}, u32[]{:S(2)}, u32[]{:S(2)}) collective-permute-start(bf16[2,128,1024]{2,1,0:T(8,128)(2,1)S(1)} %get-tuple-element.27), channel_id=1, source_target_pairs={{0,1},{1,0},{2,3},{3,2},{4,5},{5,4},{6,7},{7,6},{8,9},{9,8},{10,11... | collective-permute-start | bytes 1572872 | tf_op jit(solution)/shard_map/ppermute | solution.py:313
  45.0 8.4 %collective-permute-start.1 = (bf16[2,128,1024]{2,1,0:T(8,128)(2,1)S(1)}, bf16[2,128,1024]{2,1,0:T(8,128)(2,1)S(1)}, u32[]{:S(2)}, u32[]{:S(2)}) collective-permute-start(bf16[2,128,1024]{2,1,0:T(8,128)(2,1)S(1)} %shard_map.53), channel_id=1, source_target_pairs={{0,1},{1,0},{2,3},{3,2},{4,5},{5,4},{6,7},{7,6},{8,9},{9,8},{10,11... | collective-permute-start | bytes 1572872 | tf_op jit(solution)/shard_map/ppermute | solution.py:313
  45.6 7.8 %collective-permute-start.2 = (bf16[2,128,768]{2,1,0:T(8,128)(2,1)S(1)}, bf16[2,128,768]{2,1,0:T(8,128)(2,1)S(1)}, u32[]{:S(2)}, u32[]{:S(2)}) collective-permute-start(bf16[2,128,768]{2,1,0:T(8,128)(2,1)S(1)} %get-tuple-element.33), channel_id=1, source_target_pairs={{0,2},{1,7},{2,0},{3,5},{4,6},{5,3},{6,4},{7,1},{8,10},{9,15},{10,... | collective-permute-start | bytes 1179656 | tf_op jit(solution)/shard_map/ppermute | solution.py:313
  47.2 9.4 %collective-permute-start.3 = (bf16[2,128,256]{2,1,0:T(8,128)(2,1)S(1)}, bf16[2,128,256]{2,1,0:T(8,128)(2,1)S(1)}, u32[]{:S(2)}, u32[]{:S(2)}) collective-permute-start(bf16[2,128,256]{2,1,0:T(8,128)(2,1)S(1)} %get-tuple-element.35), channel_id=1, source_target_pairs={{0,2},{1,7},{2,0},{3,5},{4,6},{5,3},{6,4},{7,1},{8,10},{9,15},{10,... | collective-permute-start | bytes 393224 | tf_op jit(solution)/shard_map/ppermute | solution.py:313
  53.5 8.7 %collective-permute-start.4 = (bf16[128,768]{1,0:T(8,128)(2,1)S(1)}, bf16[128,768]{1,0:T(8,128)(2,1)S(1)}, u32[]{:S(2)}, u32[]{:S(2)}) collective-permute-start(bf16[128,768]{1,0:T(8,128)(2,1)S(1)} %get-tuple-element.37), channel_id=1, source_target_pairs={{0,6},{1,3},{2,4},{3,1},{4,2},{5,7},{6,0},{7,5},{8,14},{9,11},{10,... | collective-permute-start | bytes 589832 | tf_op jit(solution)/shard_map/ppermute | solution.py:313
  56.7 5.6 %collective-permute-start.5 = (bf16[128,256]{1,0:T(8,128)(2,1)S(1)}, bf16[128,256]{1,0:T(8,128)(2,1)S(1)}, u32[]{:S(2)}, u32[]{:S(2)}) collective-permute-start(bf16[128,256]{1,0:T(8,128)(2,1)S(1)} %get-tuple-element.38), channel_id=1, source_target_pairs={{0,6},{1,3},{2,4},{3,1},{4,2},{5,7},{6,0},{7,5},{8,14},{9,11},{10,... | collective-permute-start | bytes 196616 | tf_op jit(solution)/shard_map/ppermute | solution.py:313

commit v3 on v2

--- a/solution.py
+++ b/solution.py
@@ -13,7 +13,7 @@
 HBM = pl.BlockSpec(memory_space=pltpu.HBM)
 
 EDGE = 8
-SPLIT = (0, 768, 1024)
+SPLIT = (0, 512, 1024)
 CHUNKS = len(SPLIT) - 1
 
 
@@ -45,7 +45,17 @@
     return total
 
 
-def pack_kernel(x_hbm, sf_hbm, out_hbm, x_ref, head_ref, tail_ref, sf_ref, out_ref, sems, *, gsize):
+def short_conv_rows(x, rows_ref, sf_ref, feature, lanes):
+    tokens = x.shape[0]
+    rows_ref[:8, :] = jnp.zeros((8, x.shape[1]), F32)
+    rows_ref[8:, :] = x
+    total = sf_ref[feature, 0:1, lanes] * x
+    for d in range(1, sf_ref.shape[1]):
+        total = total + sf_ref[feature, d : d + 1, lanes] * rows_ref[8 - d : 8 - d + tokens, :]
+    return total
+
+
+def pack_kernel(x_hbm, sf_hbm, out_hbm, x_ref, head_ref, tail_ref, sf_ref, out_ref, rows_ref, sems, *, gsize):
     feats, tokens, channels = x_hbm.shape
     parts = channels // 128
     few = 128 // gsize
@@ -77,7 +87,8 @@
         groups = slice(j * few, (j + 1) * few)
         reads[j].wait()
         x = [x_ref[f, :, lanes].astype(F32) for f in range(feats - 1)]
-        values = short_conv(x[0], sf_ref, 1, lanes) * short_conv(x[1], sf_ref, 2, lanes)
+        key = short_conv_rows(x[0], rows_ref.at[j, 0], sf_ref, 1, lanes)
+        values = key * short_conv_rows(x[1], rows_ref.at[j, 1], sf_ref, 2, lanes)
         out_ref[groups, :gsize, :] = values.T.astype(BF).reshape(few, gsize, tokens)
         edges = [tail_ref[:, lanes].astype(F32), head_ref[:, lanes].astype(F32)]
         for f in range(feats - 1):
@@ -89,7 +100,50 @@
         copy.wait()
 
 
-def prep_kernel(x_hbm, sf_hbm, lf_hbm, g_ref, gate_ref, coef_ref, x_ref, sf_ref, lf_ref, sems, *, gsize):
+def pieces_of(first, own):
+    tp = lax.axis_index("tp")
+    y = lax.div(tp, 2)
+    core = lax.rem(tp, 2)
+    if not own:
+        core = 1 - core
+    near = jnp.bitwise_xor(y, 1)
+    far = 3 - y
+    slots = []
+    for slot in range(2):
+        row = []
+        for chunk in range(CHUNKS):
+            even = lax.rem(core + chunk, 2) == 0
+            if first:
+                chip = jnp.where(even, near, far) if slot == 0 else 3 - near
+            else:
+                chip = y if slot == 0 else jnp.where(even, far, near)
+            row.append(chip * 2 + core)
+        slots.append(row)
+    return slots
+
+
+def fetches(w_hbm, w_ref, sems, wanted):
+    cols = w_ref.shape[2]
+    copies = []
+    for slot, row in enumerate(wanted):
+        for chunk, block in enumerate(row):
+            low, high = SPLIT[chunk], SPLIT[chunk + 1]
+            start = pl.multiple_of(block * cols + low, 128)
+            copies.append(
+                pltpu.make_async_copy(
+                    w_hbm.at[:, pl.ds(start, high - low)],
+                    w_ref.at[slot, :, low:high],
+                    sems.at[slot * CHUNKS + chunk],
+                )
+            )
+    for copy in copies:
+        copy.start()
+    return copies
+
+
+def prep_kernel(
+    x_hbm, sf_hbm, lf_hbm, w_hbm, g_ref, gate_ref, coef_ref, w_ref, x_ref, sf_ref, lf_ref, sems, w_sems, *, gsize
+):
     tok, channels = x_ref.shape
     _, taps, _ = sf_ref.shape
     groups, reach = lf_ref.shape
@@ -101,6 +155,7 @@
     ]
     for copy in copies:
         copy.start()
+    fetched = fetches(w_hbm, w_ref, w_sems, pieces_of(True, False))
     me = lax.axis_index("ctx")
     for copy in copies:
         copy.wait()
@@ -127,46 +182,17 @@
             here = pltpu.roll(jnp.broadcast_to(taps_k, (tok, tok)), 0, 1, stride=1, stride_axis=0)
         else:
             here = jnp.zeros((tok, tok), F32)
-        block = jnp.where(upper, here, before).astype(BF)
-        g_ref[k * tok : (k + 1) * tok, tok:] = block
-        g_ref[(k + 1) * tok : (k + 2) * tok, :tok] = block
+        g_ref[k * tok : (k + 1) * tok, :] = jnp.where(upper, here, before).astype(BF)
         before = here
-    g_ref[:tok, :tok] = jnp.zeros((tok, tok), BF)
-    g_ref[lags * tok :, tok:] = jnp.zeros((tok, tok), BF)
     for j in range(0, channels, 128):
         lanes = slice(j, j + 128)
         gate_ref[:, lanes] = short_conv(x_ref[:, lanes].astype(F32), sf_ref, 0, lanes)
-
-
-def blocks_of(first, own):
-    tp = lax.axis_index("tp")
-    y = lax.div(tp, 2)
-    core = lax.rem(tp, 2)
-    if not own:
-        core = 1 - core
-    near = jnp.bitwise_xor(y, 1)
-    far = 3 - y
-    even = core == 0
-    if first:
-        chips = (jnp.where(even, near, far), 3 - near)
-    else:
-        chips = (y, jnp.where(even, far, near))
-    return [chip * 2 + core for chip in chips]
-
-
-def fetches(w_hbm, w_ref, sems, wanted):
-    cols = w_ref.shape[2]
-    copies = []
-    for slot, block in enumerate(wanted):
-        start = pl.multiple_of(block * cols, cols)
-        copies.append(pltpu.make_async_copy(w_hbm.at[:, pl.ds(start, cols)], w_ref.at[slot], sems.at[slot]))
-    for copy in copies:
-        copy.start()
-    return copies
-
-
-def conv_kernel(x_ref, g_ref, coef_ref, w_hbm, out_ref, w_ref, z_ref, sems, *, gsize):
-    copies = fetches(w_hbm, w_ref, sems, blocks_of(True, False) + blocks_of(True, True))
+    for copy in fetched:
+        copy.wait()
+
+
+def conv_kernel(x_ref, t_ref, coef_ref, w_hbm, out_ref, w_ref, z_ref, g_ref, sems, *, gsize):
+    copies = fetches(w_hbm, w_ref, sems, pieces_of(True, True)[:1])
     blocks, _, tok = x_ref.shape
     taps = coef_ref.shape[0]
     lane = lax.broadcasted_iota(jnp.int32, (blocks, 8, tok), 2)
@@ -187,6 +213,10 @@
     value = jnp.concatenate([at(5 * EDGE), at(64 + 5 * EDGE)], axis=1)
     head = lax.broadcasted_iota(jnp.int32, (blocks, gsize, tok), 2) < EDGE
     values = jnp.where(head, key * value, x_ref[:, :gsize, :].astype(F32))
+    g_ref[:tok, :tok] = jnp.zeros((tok, tok), BF)
+    g_ref[tok:, :tok] = t_ref[...]
+    g_ref[: t_ref.shape[0], tok:] = t_ref[...]
+    g_ref[t_ref.shape[0] :, tok:] = jnp.zeros((tok, tok), BF)
     values = values.astype(BF).reshape(blocks // 2, 2, gsize, tok)
     rows = blocks // 2 * gsize
     for k in range(g_ref.shape[0] // tok):
@@ -214,17 +244,20 @@
         out_ref[slot] = product(ht_ref[...], w_ref[slot])
 
 
-def first_own_kernel(ht_ref, w_ref, w_hbm, out_ref, last_ref, sems):
-    copies = fetches(w_hbm, last_ref, sems, blocks_of(False, False) + blocks_of(False, True))
+def first_own_kernel(ht_ref, w_ref, w_hbm, out_ref, rest_ref, sems):
+    copies = fetches(w_hbm, rest_ref, sems, pieces_of(True, True)[1:])
+    out_ref[0] = product(ht_ref[...], w_ref[0])
+    for copy in copies:
+        copy.wait()
+    out_ref[1] = product(ht_ref[...], rest_ref[0])
+
+
+def last_kernel(ht_ref, w_hbm, out_ref, w_ref, sems, *, own):
+    copies = fetches(w_hbm, w_ref, sems, pieces_of(False, own))
     for slot in range(2):
-        out_ref[slot] = product(ht_ref[...], w_ref[slot + 2])
-    for copy in copies:
-        copy.wait()
-
-
-def last_kernel(ht_ref, w_ref, out_ref, *, first):
-    for slot in range(2):
-        out_ref[slot] = product(ht_ref[...], w_ref[first + slot])
+        for copy in copies[slot * CHUNKS : (slot + 1) * CHUNKS]:
+            copy.wait()
+        out_ref[slot] = product(ht_ref[...], w_ref[slot])
 
 
 def join_kernel(got_ref, own_ref, ht_in_ref, out_ref, ht_ref, *, chunk):
@@ -261,6 +294,7 @@
 
     x = in_hbm(projected.transpose(1, 0, 2))
     sf = in_hbm(short_filter.transpose(1, 0, 2))
+    weight = in_hbm(out_weight)
     packed = call(
         functools.partial(pack_kernel, gsize=gsize),
         shaped((groups, gsize + 8, tok)),
@@ -271,43 +305,50 @@
             pltpu.VMEM((EDGE, channels), BF),
             pltpu.VMEM((feats, taps, channels), F32),
             pltpu.VMEM((groups, gsize + 8, tok), BF),
+            pltpu.VMEM((channels // 128, feats - 1, tok + 8, 128), F32),
             pltpu.SemaphoreType.DMA((2 * channels // 128 + 3,)),
         ),
         out_specs=HBM,
     )(x, sf)
     spread = lax.all_to_all(packed, "ctx", 0, 0, tiled=True)
-    toeplitz, gate, coef = call(
+    toeplitz, gate, coef, theirs_weight = call(
         functools.partial(prep_kernel, gsize=gsize),
         [
-            shaped(((lags + 1) * tok, 2 * tok)),
+            shaped((lags * tok, tok)),
             shaped((tok, channels), F32),
             shaped((taps, 8, 128), F32),
+            shaped((2, channels, cols)),
         ],
-        [HBM] * 3,
+        [HBM] * 4,
         scratch=(
             pltpu.VMEM((tok, channels), BF),
             pltpu.VMEM((feats, taps, channels), F32),
             pltpu.VMEM(long_filter.shape, BF),
             pltpu.SemaphoreType.DMA((3,)),
+            pltpu.SemaphoreType.DMA((2 * CHUNKS,)),
         ),
-    )(x, sf, in_hbm(long_filter))
-    weight = in_hbm(out_weight)
-    mixed, first_weight = call(
+    )(x, sf, in_hbm(long_filter), weight)
+    mixed, own_weight = call(
         functools.partial(conv_kernel, gsize=gsize),
-        [shaped((blocks, gsize, tok)), shaped((4, channels, cols))],
+        [shaped((blocks, gsize, tok)), shaped((1, channels, cols))],
         [VMEM] * 3 + [HBM],
-        scratch=(pltpu.VMEM((blocks // 2 * gsize, (lags + 1) * tok), BF), pltpu.SemaphoreType.DMA((4,))),
+        scratch=(
+            pltpu.VMEM((blocks // 2 * gsize, (lags + 1) * tok), BF),
+            pltpu.VMEM(((lags + 1) * tok, 2 * tok), BF),
+            pltpu.SemaphoreType.DMA((CHUNKS,)),
+        ),
     )(spread, toeplitz, coef, weight)
     mixed = lax.all_to_all(mixed, "ctx", 0, 0, tiled=True).reshape(channels, tok)
 
-    def project_last(ht, first):
+    def project_last(ht, own):
         return call(
-            functools.partial(last_kernel, first=first),
+            functools.partial(last_kernel, own=own),
             shaped((2, tok, cols)),
-            [VMEM] * 2,
+            [VMEM, HBM],
+            scratch=(pltpu.VMEM((2, channels, cols), BF), pltpu.SemaphoreType.DMA((2 * CHUNKS,))),
             flops=4 * tok * channels * cols,
             nbytes=4 * channels * cols,
-        )(ht, last_weight)
+        )(ht, weight)
 
     def swap(x, peer):
         return lax.ppermute(x, "tp", [(i, peer(i)) for i in range(n_tp)])
@@ -315,32 +356,31 @@
     def partner(i):
         return i ^ 1
 
-    def hop_one(i):
-        return i ^ 2 if i % 2 == 0 else 8 - i
-
-    def hop_two(i):
-        return 6 - i if i % 2 == 0 else i ^ 2
+    def hop(i, parity):
+        return i ^ 2 if (i + parity) % 2 == 0 else (3 - i // 2) * 2 + i % 2
 
     widths = [SPLIT[i + 1] - SPLIT[i] for i in range(CHUNKS)]
     theirs, ht = call(
         first_theirs_kernel, [shaped((2, tok, cols)), shaped((tok, channels))], [VMEM] * 3
-    )(mixed, gate, first_weight)
+    )(mixed, gate, theirs_weight)
     got = swap(theirs, partner)
-    own, last_weight = call(
+    own = call(
         first_own_kernel,
-        [shaped((2, tok, cols)), shaped((4, channels, cols))],
+        shaped((2, tok, cols)),
         [VMEM] * 2 + [HBM],
-        scratch=(pltpu.SemaphoreType.DMA((4,)),),
-    )(ht, first_weight, weight)
+        scratch=(pltpu.VMEM((1, channels, cols), BF), pltpu.SemaphoreType.DMA((CHUNKS,))),
+    )(ht, own_weight, weight)
     arrived = []
     for i in range(CHUNKS):
         send, ht = call(
-            functools.partial(join_kernel, chunk=i), [shaped((2, tok, widths[i])), shaped((tok, channels))], [VMEM] * 3
+            functools.partial(join_kernel, chunk=i),
+            [shaped((2, tok, widths[i])), shaped((tok, channels))],
+            [VMEM] * 3,
         )(got, own, ht)
-        arrived.append(swap(send, hop_one))
-    theirs = project_last(ht, 0)
+        arrived.append(swap(send, functools.partial(hop, parity=i)))
+    theirs = project_last(ht, False)
     got = swap(theirs, partner)
-    own = project_last(ht, 2)
+    own = project_last(ht, True)
     kept, last = [], []
     for i in range(CHUNKS):
         onward, keep = call(
@@ -349,7 +389,7 @@
             [VMEM] * (3 + min(i, 1)),
         )(got, own, arrived[i], *kept[-1:])
         kept.append(keep)
-        last.append(swap(onward, hop_two))
+        last.append(swap(onward, functools.partial(hop, parity=i + 1)))
     return call(finish_kernel, shaped((tok, cols)), [VMEM] * (2 * CHUNKS))(*kept, *last)
 
 

time: 63.3 us -> 64.4 us (1.017)
  the two profiles are of different devices: /device:TPU:2 before, /device:TPU:1 now
where the time goes in v3:
time: 64.4 us; the launch traced here: 64 us
  starting transfers between devices  19.6 us (30%)
  waiting for transfers between devices  16.9 us (26%)
  blocking collectives  14.4 us (22%)
  Pallas kernels  13 us (20%)
    all_to_all x1, blocking collectives, body(): lax.all_to_all(mixed, 'ctx', 0, 0, tiled=True).reshape(channels, tok)  14.4 us
    all_to_all x1, starting transfers between devices, body(): spread = lax.all_to_all(packed, 'ctx', 0, 0, tiled=True)  11.9 us
    ppermute x6, waiting for transfers between devices, swap(): return lax.ppermute(x, 'tp', [(i, peer(i)) for i in range(n_tp)])  9.51 us
    ppermute x6, starting transfers between devices, swap(): return lax.ppermute(x, 'tp', [(i, peer(i)) for i in range(n_tp)])  7.77 us
    all_to_all x1, waiting for transfers between devices, body(): spread = lax.all_to_all(packed, 'ctx', 0, 0, tiled=True)  7.34 us
    pallas_call x2, Pallas kernels, project_last(): call(functools.partial(last_kernel, own=own), shaped((2, tok, cols)), [VM...  3.77 us
    pallas_call x1, Pallas kernels, body(): call(functools.partial(pack_kernel, gsize=gsize), shaped((groups, gsize +...  2.21 us
    pallas_call x1, Pallas kernels, body(): call(functools.partial(prep_kernel, gsize=gsize), [shaped((lags * tok, to...  2.04 us
  transfers between devices with their start and end apart: 7, of which 5 were waited for; matrix products, arithmetic and copies ran while one was open for 0% of the time, Pallas kernels for 9%

profile of v3, /device:TPU:1, one launch (start us, length us, event | category | flops | bytes accessed | tf_op | source)
XLA Modules:
  0.0 64.0 jit_solution(12830899984574884818)
XLA Ops:
  0.0 2.2 %shard_map.46 = bf16[32,24,128]{2,1,0:T(8,128)(2,1)} custom-call(bf16[3,128,512]{2,1,0:T(8,128)(2,1)} %bitcast.4, f32[3,7,512]{2,1,0:T(8,128)} %bitcast.6), custom_call_target="tpu_custom_call" | custom-call | tf_op jit(solution)/shard_map/pallas_call | solution.py:298
  2.2 11.9 %all-to-all-start = ((bf16[32,24,128]{2,1,0:T(8,128)(2,1)}), bf16[32,24,128]{2,1,0:T(8,128)(2,1)S(1)}, u32[]{:S(2)}, u32[]{:S(2)}) async-start(bf16[32,24,128]{2,1,0:T(8,128)(2,1)} %shard_map.46), calls=%async_computation | async-start | bytes 393216 | tf_op jit(solution)/shard_map/all_to_all | solution.py:313
  14.1 2.0 %shard_map.47 = (bf16[2176,128]{1,0:T(8,128)(2,1)S(1)}, f32[128,512]{1,0:T(8,128)S(1)}, f32[7,8,128]{2,1,0:T(8,128)S(1)}, bf16[2,512,1024]{2,1,0:T(8,128)(2,1)S(1)}) custom-call(bf16[3,128,512]{2,1,0:T(8,128)(2,1)} %bitcast.5, f32[3,7,512]{2,1,0:T(8,128)} %bitcast.7, bf16[32,2048]{1,0:T(8,128)(2,1)} %lf_hbm.1, bf16[512,8192]{1,0:T(8,128)(2,1)} %w_hbm.9), custom_call_target="tpu_custom_call" | custom-call | tf_op jit(solution)/shard_map/pallas_call | solution.py:314
  16.1 7.3 %all-to-all-done.x_ref = bf16[32,24,128]{2,1,0:T(8,128)(2,1)S(1)} async-done(((bf16[32,24,128]{2,1,0:T(8,128)(2,1)}), bf16[32,24,128]{2,1,0:T(8,128)(2,1)S(1)}, u32[]{:S(2)}, u32[]{:S(2)}) %all-to-all-start) | async-done | bytes 196640 | tf_op jit(solution)/shard_map/all_to_all | solution.py:313
  23.5 1.7 %shard_map.48 = (bf16[32,16,128]{2,1,0:T(8,128)(2,1)S(1)}, bf16[1,512,1024]{2,1,0:T(8,128)(2,1)S(1)}) custom-call(bf16[32,24,128]{2,1,0:T(8,128)(2,1)S(1)} %all-to-all-done.x_ref, bf16[2176,128]{1,0:T(8,128)(2,1)S(1)} %get-tuple-element.21.t_ref, f32[7,8,128]{2,1,0:T(8,128)S(1)} %get-tuple-element.22.coef_ref, bf16[512,8192]{1,0:T(8,128)(2,1)} %w_hbm.9), custom_call_target="tpu_custom_call" | custom-call | tf_op jit(solution)/shard_map/pallas_call | solution.py:331
  25.2 14.4 %all_to_all.10 = bf16[32,16,128]{2,1,0:T(8,128)(2,1)S(1)} all-to-all(bf16[32,16,128]{2,1,0:T(8,128)(2,1)S(1)} %get-tuple-element.23), channel_id=1, replica_groups=mesh['ctx'=32,'tp'=8] {'ctx'}, dimensions={0} | all-to-all | bytes 262144 | tf_op jit(solution)/shard_map/all_to_all | solution.py:341
  39.6 0.5 shard_map.49
  40.1 2.9 %collective-permute-start = (bf16[2,128,1024]{2,1,0:T(8,128)(2,1)S(1)}, bf16[2,128,1024]{2,1,0:T(8,128)(2,1)S(1)}, u32[]{:S(2)}, u32[]{:S(2)}) collective-permute-start(bf16[2,128,1024]{2,1,0:T(8,128)(2,1)S(1)} %get-tuple-element.26), channel_id=1, source_target_pairs={{0,1},{1,0},{2,3},{3,2},{4,5},{5,4},{6,7},{7,6},{8,9},{9,8},{10,11... | collective-permute-start | bytes 1572872 | tf_op jit(solution)/shard_map/ppermute | solution.py:354
  43.0 1.7 %shard_map.50.own_ref = bf16[2,128,1024]{2,1,0:T(8,128)(2,1)S(1)} custom-call(bf16[128,512]{1,0:T(8,128)(2,1)S(1)} %get-tuple-element.27.ht_ref.ht_in_ref, bf16[1,512,1024]{2,1,0:T(8,128)(2,1)S(1)} %get-tuple-element.28.w_ref, bf16[512,8192]{1,0:T(8,128)(2,1)} %w_hbm.9), custom_call_target="tpu_custom_call" | custom-call | tf_op jit(solution)/shard_map/pallas_call | solution.py:367
  44.8 0.0 collective-permute-done.got_ref
  44.8 0.1 shard_map.51
  44.9 0.1 shard_map.52
  44.9 1.9 %shard_map.53 = bf16[2,128,1024]{2,1,0:T(8,128)(2,1)S(1)} custom-call(bf16[128,512]{1,0:T(8,128)(2,1)S(1)} %get-tuple-element.30.ht_ref, bf16[512,8192]{1,0:T(8,128)(2,1)} %w_hbm.9), custom_call_target="tpu_custom_call" | custom-call | flops 268435456 | bytes 2097152 | tf_op jit(solution)/shard_map/pallas_call | solution.py:344
  46.8 0.3 collective-permute-start.1
  47.1 2.7 %collective-permute-start.2 = (bf16[2,128,512]{2,1,0:T(8,128)(2,1)S(1)}, bf16[2,128,512]{2,1,0:T(8,128)(2,1)S(1)}, u32[]{:S(2)}, u32[]{:S(2)}) collective-permute-start(bf16[2,128,512]{2,1,0:T(8,128)(2,1)S(1)} %get-tuple-element.31), channel_id=1, source_target_pairs={{0,2},{1,7},{2,0},{3,5},{4,6},{5,3},{6,4},{7,1},{8,10},{9,15},{10,... | collective-permute-start | bytes 786440 | tf_op jit(solution)/shard_map/ppermute | solution.py:354
  49.8 1.9 %shard_map.54.own_ref = bf16[2,128,1024]{2,1,0:T(8,128)(2,1)S(1)} custom-call(bf16[128,512]{1,0:T(8,128)(2,1)S(1)} %get-tuple-element.30.ht_ref, bf16[512,8192]{1,0:T(8,128)(2,1)} %w_hbm.9), custom_call_target="tpu_custom_call" | custom-call | flops 268435456 | bytes 2097152 | tf_op jit(solution)/shard_map/pallas_call | solution.py:344
  51.7 2.7 %collective-permute-done.2.in_ref = bf16[2,128,512]{2,1,0:T(8,128)(2,1)S(1)} collective-permute-done((bf16[2,128,512]{2,1,0:T(8,128)(2,1)S(1)}, bf16[2,128,512]{2,1,0:T(8,128)(2,1)S(1)}, u32[]{:S(2)}, u32[]{:S(2)}) %collective-permute-start.2) | collective-permute-done | bytes 262176 | tf_op jit(solution)/shard_map/ppermute | solution.py:354
  54.4 0.1 shard_map.55
  54.5 1.7 %collective-permute-done.3.in_ref = bf16[2,128,512]{2,1,0:T(8,128)(2,1)S(1)} collective-permute-done((bf16[2,128,512]{2,1,0:T(8,128)(2,1)S(1)}, bf16[2,128,512]{2,1,0:T(8,128)(2,1)S(1)}, u32[]{:S(2)}, u32[]{:S(2)}) %collective-permute-start.3) | collective-permute-done | bytes 262176 | tf_op jit(solution)/shard_map/ppermute | solution.py:354
  56.2 0.1 shard_map.56
  56.3 1.8 %collective-permute-start.5 = (bf16[128,512]{1,0:T(8,128)(2,1)S(1)}, bf16[128,512]{1,0:T(8,128)(2,1)S(1)}, u32[]{:S(2)}, u32[]{:S(2)}) collective-permute-start(bf16[128,512]{1,0:T(8,128)(2,1)S(1)} %get-tuple-element.36), channel_id=1, source_target_pairs={{0,2},{1,7},{2,0},{3,5},{4,6},{5,3},{6,4},{7,1},{8,10},{9,15},{10,... | collective-permute-start | bytes 393224 | tf_op jit(solution)/shard_map/ppermute | solution.py:354
  58.1 3.3 %collective-permute-done.5.refs_3_ = bf16[128,512]{1,0:T(8,128)(2,1)S(1)} collective-permute-done((bf16[128,512]{1,0:T(8,128)(2,1)S(1)}, bf16[128,512]{1,0:T(8,128)(2,1)S(1)}, u32[]{:S(2)}, u32[]{:S(2)}) %collective-permute-start.5) | collective-permute-done | bytes 131104 | tf_op jit(solution)/shard_map/ppermute | solution.py:354
  61.4 1.8 %collective-permute-done.4.refs_2_ = bf16[128,512]{1,0:T(8,128)(2,1)S(1)} collective-permute-done((bf16[128,512]{1,0:T(8,128)(2,1)S(1)}, bf16[128,512]{1,0:T(8,128)(2,1)S(1)}, u32[]{:S(2)}, u32[]{:S(2)}) %collective-permute-start.4) | collective-permute-done | bytes 131104 | tf_op jit(solution)/shard_map/ppermute | solution.py:354
  63.3 0.7 %shard_map.57 = bf16[128,1024]{1,0:T(8,128)(2,1)} custom-call(f32[128,512]{1,0:T(8,128)S(1)} %get-tuple-element.32.refs_0_, f32[128,512]{1,0:T(8,128)S(1)} %get-tuple-element.34.refs_1_, bf16[128,512]{1,0:T(8,128)(2,1)S(1)} %collective-permute-done.4.refs_2_, bf16[128,512]{1,0:T(8,128)(2,1)S(1)} %collective-permute-done.5.refs_3_), custom_call_target="tpu_custom_call" | custom-call | tf_op jit(solution)/shard_map/pallas_call | solution.py:393
  (3 shorter events, 0.0 us)
Async XLA Ops:
  2.2 21.3 %all-to-all-start = ((bf16[32,24,128]{2,1,0:T(8,128)(2,1)}), bf16[32,24,128]{2,1,0:T(8,128)(2,1)S(1)}, u32[]{:S(2)}, u32[]{:S(2)}) async-start(bf16[32,24,128]{2,1,0:T(8,128)(2,1)} %shard_map.46), calls=%async_computation | async-start | bytes 393216 | tf_op jit(solution)/shard_map/all_to_all | solution.py:313
  40.1 4.6 %collective-permute-start = (bf16[2,128,1024]{2,1,0:T(8,128)(2,1)S(1)}, bf16[2,128,1024]{2,1,0:T(8,128)(2,1)S(1)}, u32[]{:S(2)}, u32[]{:S(2)}) collective-permute-start(bf16[2,128,1024]{2,1,0:T(8,128)(2,1)S(1)} %get-tuple-element.26), channel_id=1, source_target_pairs={{0,1},{1,0},{2,3},{3,2},{4,5},{5,4},{6,7},{7,6},{8,9},{9,8},{10,11... | collective-permute-start | bytes 1572872 | tf_op jit(solution)/shard_map/ppermute | solution.py:354
  46.8 7.6 %collective-permute-start.1 = (bf16[2,128,1024]{2,1,0:T(8,128)(2,1)S(1)}, bf16[2,128,1024]{2,1,0:T(8,128)(2,1)S(1)}, u32[]{:S(2)}, u32[]{:S(2)}) collective-permute-start(bf16[2,128,1024]{2,1,0:T(8,128)(2,1)S(1)} %shard_map.53), channel_id=1, source_target_pairs={{0,1},{1,0},{2,3},{3,2},{4,5},{5,4},{6,7},{7,6},{8,9},{9,8},{10,11... | collective-permute-start | bytes 1572872 | tf_op jit(solution)/shard_map/ppermute | solution.py:354
  47.1 7.3 %collective-permute-start.2 = (bf16[2,128,512]{2,1,0:T(8,128)(2,1)S(1)}, bf16[2,128,512]{2,1,0:T(8,128)(2,1)S(1)}, u32[]{:S(2)}, u32[]{:S(2)}) collective-permute-start(bf16[2,128,512]{2,1,0:T(8,128)(2,1)S(1)} %get-tuple-element.31), channel_id=1, source_target_pairs={{0,2},{1,7},{2,0},{3,5},{4,6},{5,3},{6,4},{7,1},{8,10},{9,15},{10,... | collective-permute-start | bytes 786440 | tf_op jit(solution)/shard_map/ppermute | solution.py:354
  49.8 6.4 %collective-permute-start.3 = (bf16[2,128,512]{2,1,0:T(8,128)(2,1)S(1)}, bf16[2,128,512]{2,1,0:T(8,128)(2,1)S(1)}, u32[]{:S(2)}, u32[]{:S(2)}) collective-permute-start(bf16[2,128,512]{2,1,0:T(8,128)(2,1)S(1)} %get-tuple-element.33), channel_id=1, source_target_pairs={{0,6},{1,3},{2,4},{3,1},{4,2},{5,7},{6,0},{7,5},{8,14},{9,11},{10,... | collective-permute-start | bytes 786440 | tf_op jit(solution)/shard_map/ppermute | solution.py:354
  56.3 5.1 %collective-permute-start.5 = (bf16[128,512]{1,0:T(8,128)(2,1)S(1)}, bf16[128,512]{1,0:T(8,128)(2,1)S(1)}, u32[]{:S(2)}, u32[]{:S(2)}) collective-permute-start(bf16[128,512]{1,0:T(8,128)(2,1)S(1)} %get-tuple-element.36), channel_id=1, source_target_pairs={{0,2},{1,7},{2,0},{3,5},{4,6},{5,3},{6,4},{7,1},{8,10},{9,15},{10,... | collective-permute-start | bytes 393224 | tf_op jit(solution)/shard_map/ppermute | solution.py:354
  58.1 5.1 %collective-permute-start.4 = (bf16[128,512]{1,0:T(8,128)(2,1)S(1)}, bf16[128,512]{1,0:T(8,128)(2,1)S(1)}, u32[]{:S(2)}, u32[]{:S(2)}) collective-permute-start(bf16[128,512]{1,0:T(8,128)(2,1)S(1)} %get-tuple-element.35), channel_id=1, source_target_pairs={{0,6},{1,3},{2,4},{3,1},{4,2},{5,7},{6,0},{7,5},{8,14},{9,11},{10,... | collective-permute-start | bytes 393224 | tf_op jit(solution)/shard_map/ppermute | solution.py:354

commit v4 on v3

--- a/solution.py
+++ b/solution.py
@@ -13,7 +13,7 @@
 HBM = pl.BlockSpec(memory_space=pltpu.HBM)
 
 EDGE = 8
-SPLIT = (0, 512, 1024)
+SPLIT = (0, 640, 1024)
 CHUNKS = len(SPLIT) - 1
 
 
@@ -100,7 +100,7 @@
         copy.wait()
 
 
-def pieces_of(first, own):
+def blocks_of(first, own):
     tp = lax.axis_index("tp")
     y = lax.div(tp, 2)
     core = lax.rem(tp, 2)
@@ -108,34 +108,20 @@
         core = 1 - core
     near = jnp.bitwise_xor(y, 1)
     far = 3 - y
-    slots = []
-    for slot in range(2):
-        row = []
-        for chunk in range(CHUNKS):
-            even = lax.rem(core + chunk, 2) == 0
-            if first:
-                chip = jnp.where(even, near, far) if slot == 0 else 3 - near
-            else:
-                chip = y if slot == 0 else jnp.where(even, far, near)
-            row.append(chip * 2 + core)
-        slots.append(row)
-    return slots
+    even = core == 0
+    if first:
+        chips = (jnp.where(even, near, far), 3 - near)
+    else:
+        chips = (y, jnp.where(even, far, near))
+    return [chip * 2 + core for chip in chips]
 
 
 def fetches(w_hbm, w_ref, sems, wanted):
     cols = w_ref.shape[2]
     copies = []
-    for slot, row in enumerate(wanted):
-        for chunk, block in enumerate(row):
-            low, high = SPLIT[chunk], SPLIT[chunk + 1]
-            start = pl.multiple_of(block * cols + low, 128)
-            copies.append(
-                pltpu.make_async_copy(
-                    w_hbm.at[:, pl.ds(start, high - low)],
-                    w_ref.at[slot, :, low:high],
-                    sems.at[slot * CHUNKS + chunk],
-                )
-            )
+    for slot, block in enumerate(wanted):
+        start = pl.multiple_of(block * cols, cols)
+        copies.append(pltpu.make_async_copy(w_hbm.at[:, pl.ds(start, cols)], w_ref.at[slot], sems.at[slot]))
     for copy in copies:
         copy.start()
     return copies
@@ -155,7 +141,7 @@
     ]
     for copy in copies:
         copy.start()
-    fetched = fetches(w_hbm, w_ref, w_sems, pieces_of(True, False))
+    fetched = fetches(w_hbm, w_ref, w_sems, blocks_of(True, False))
     me = lax.axis_index("ctx")
     for copy in copies:
         copy.wait()
@@ -191,8 +177,7 @@
         copy.wait()
 
 
-def conv_kernel(x_ref, t_ref, coef_ref, w_hbm, out_ref, w_ref, z_ref, g_ref, sems, *, gsize):
-    copies = fetches(w_hbm, w_ref, sems, pieces_of(True, True)[:1])
+def conv_kernel(x_ref, t_ref, coef_ref, out_ref, z_ref, g_ref, *, gsize):
     blocks, _, tok = x_ref.shape
     taps = coef_ref.shape[0]
     lane = lax.broadcasted_iota(jnp.int32, (blocks, 8, tok), 2)
@@ -228,8 +213,6 @@
     mixed = jnp.dot(z_ref[...], g_ref[...], preferred_element_type=F32).reshape(blocks // 2, gsize, 2 * tok)
     mixed = jnp.stack([mixed[:, :, :tok], mixed[:, :, tok:]], axis=1).reshape(blocks, gsize, tok)
     out_ref[...] = jnp.where(head, gate * mixed, mixed).astype(BF)
-    for copy in copies:
-        copy.wait()
 
 
 def product(ht, weight):
@@ -244,19 +227,10 @@
         out_ref[slot] = product(ht_ref[...], w_ref[slot])
 
 
-def first_own_kernel(ht_ref, w_ref, w_hbm, out_ref, rest_ref, sems):
-    copies = fetches(w_hbm, rest_ref, sems, pieces_of(True, True)[1:])
-    out_ref[0] = product(ht_ref[...], w_ref[0])
-    for copy in copies:
-        copy.wait()
-    out_ref[1] = product(ht_ref[...], rest_ref[0])
-
-
-def last_kernel(ht_ref, w_hbm, out_ref, w_ref, sems, *, own):
-    copies = fetches(w_hbm, w_ref, sems, pieces_of(False, own))
+def fetched_kernel(ht_ref, w_hbm, out_ref, w_ref, sems, *, first, own):
+    copies = fetches(w_hbm, w_ref, sems, blocks_of(first, own))
     for slot in range(2):
-        for copy in copies[slot * CHUNKS : (slot + 1) * CHUNKS]:
-            copy.wait()
+        copies[slot].wait()
         out_ref[slot] = product(ht_ref[...], w_ref[slot])
 
 
@@ -325,27 +299,26 @@
             pltpu.VMEM((feats, taps, channels), F32),
             pltpu.VMEM(long_filter.shape, BF),
             pltpu.SemaphoreType.DMA((3,)),
-            pltpu.SemaphoreType.DMA((2 * CHUNKS,)),
+            pltpu.SemaphoreType.DMA((2,)),
         ),
     )(x, sf, in_hbm(long_filter), weight)
-    mixed, own_weight = call(
+    mixed = call(
         functools.partial(conv_kernel, gsize=gsize),
-        [shaped((blocks, gsize, tok)), shaped((1, channels, cols))],
-        [VMEM] * 3 + [HBM],
+        shaped((blocks, gsize, tok)),
+        [VMEM] * 3,
         scratch=(
             pltpu.VMEM((blocks // 2 * gsize, (lags + 1) * tok), BF),
             pltpu.VMEM(((lags + 1) * tok, 2 * tok), BF),
-            pltpu.SemaphoreType.DMA((CHUNKS,)),
         ),
-    )(spread, toeplitz, coef, weight)
+    )(spread, toeplitz, coef)
     mixed = lax.all_to_all(mixed, "ctx", 0, 0, tiled=True).reshape(channels, tok)
 
-    def project_last(ht, own):
+    def project(ht, first, own):
         return call(
-            functools.partial(last_kernel, own=own),
+            functools.partial(fetched_kernel, first=first, own=own),
             shaped((2, tok, cols)),
             [VMEM, HBM],
-            scratch=(pltpu.VMEM((2, channels, cols), BF), pltpu.SemaphoreType.DMA((2 * CHUNKS,))),
+            scratch=(pltpu.VMEM((2, channels, cols), BF), pltpu.SemaphoreType.DMA((2,))),
             flops=4 * tok * channels * cols,
             nbytes=4 * channels * cols,
         )(ht, weight)
@@ -364,23 +337,16 @@
         first_theirs_kernel, [shaped((2, tok, cols)), shaped((tok, channels))], [VMEM] * 3
     )(mixed, gate, theirs_weight)
     got = swap(theirs, partner)
-    own = call(
-        first_own_kernel,
-        shaped((2, tok, cols)),
-        [VMEM] * 2 + [HBM],
-        scratch=(pltpu.VMEM((1, channels, cols), BF), pltpu.SemaphoreType.DMA((CHUNKS,))),
-    )(ht, own_weight, weight)
+    own = project(ht, True, True)
     arrived = []
     for i in range(CHUNKS):
         send, ht = call(
-            functools.partial(join_kernel, chunk=i),
-            [shaped((2, tok, widths[i])), shaped((tok, channels))],
-            [VMEM] * 3,
+            functools.partial(join_kernel, chunk=i), [shaped((2, tok, widths[i])), shaped((tok, channels))], [VMEM] * 3
         )(got, own, ht)
-        arrived.append(swap(send, functools.partial(hop, parity=i)))
-    theirs = project_last(ht, False)
+        arrived.append(swap(send, functools.partial(hop, parity=0)))
+    theirs = project(ht, False, False)
     got = swap(theirs, partner)
-    own = project_last(ht, True)
+    own = project(ht, False, True)
     kept, last = [], []
     for i in range(CHUNKS):
         onward, keep = call(
@@ -389,7 +355,7 @@
             [VMEM] * (3 + min(i, 1)),
         )(got, own, arrived[i], *kept[-1:])
         kept.append(keep)
-        last.append(swap(onward, functools.partial(hop, parity=i + 1)))
+        last.append(swap(onward, functools.partial(hop, parity=1)))
     return call(finish_kernel, shaped((tok, cols)), [VMEM] * (2 * CHUNKS))(*kept, *last)
 
 

time: 64.4 us -> 61.8 us (0.960)
  the two profiles are of different devices: /device:TPU:1 before, /device:TPU:2 now
where the time goes in v4:
time: 61.8 us; the launch traced here: 61.4 us
  starting transfers between devices  19.4 us (31%)
  waiting for transfers between devices  15.5 us (25%)
  blocking collectives  14.4 us (23%)
  Pallas kernels  12 us (19%)
    all_to_all x1, blocking collectives, body(): lax.all_to_all(mixed, 'ctx', 0, 0, tiled=True).reshape(channels, tok)  14.4 us
    all_to_all x1, starting transfers between devices, body(): spread = lax.all_to_all(packed, 'ctx', 0, 0, tiled=True)  11.6 us
    all_to_all x1, waiting for transfers between devices, body(): spread = lax.all_to_all(packed, 'ctx', 0, 0, tiled=True)  8.37 us
    ppermute x6, starting transfers between devices, swap(): return lax.ppermute(x, 'tp', [(i, peer(i)) for i in range(n_tp)])  7.76 us
    ppermute x6, waiting for transfers between devices, swap(): return lax.ppermute(x, 'tp', [(i, peer(i)) for i in range(n_tp)])  7.11 us
    pallas_call x3, Pallas kernels, project(): call(functools.partial(fetched_kernel, first=first, own=own), shaped((2,...  5.67 us
    pallas_call x1, Pallas kernels, body(): call(functools.partial(pack_kernel, gsize=gsize), shaped((groups, gsize +...  2.21 us
    pallas_call x1, Pallas kernels, body(): call(functools.partial(prep_kernel, gsize=gsize), [shaped((lags * tok, to...  1.76 us
  transfers between devices with their start and end apart: 7, of which 3 were waited for; matrix products, arithmetic and copies ran while one was open for 0% of the time, Pallas kernels for 9%

profile of v4, /device:TPU:2, one launch (start us, length us, event | category | flops | bytes accessed | tf_op | source)
XLA Modules:
  0.0 61.4 jit_solution(1278698092362441885)
XLA Ops:
  0.0 2.2 %shard_map.46 = bf16[32,24,128]{2,1,0:T(8,128)(2,1)} custom-call(bf16[3,128,512]{2,1,0:T(8,128)(2,1)} %bitcast.4, f32[3,7,512]{2,1,0:T(8,128)} %bitcast.6), custom_call_target="tpu_custom_call" | custom-call | tf_op jit(solution)/shard_map/pallas_call | solution.py:272
  2.2 11.6 %all-to-all-start = ((bf16[32,24,128]{2,1,0:T(8,128)(2,1)}), bf16[32,24,128]{2,1,0:T(8,128)(2,1)S(1)}, u32[]{:S(2)}, u32[]{:S(2)}) async-start(bf16[32,24,128]{2,1,0:T(8,128)(2,1)} %shard_map.46), calls=%async_computation | async-start | bytes 393216 | tf_op jit(solution)/shard_map/all_to_all | solution.py:287
  13.9 1.8 %shard_map.47 = (bf16[2176,128]{1,0:T(8,128)(2,1)S(1)}, f32[128,512]{1,0:T(8,128)S(1)}, f32[7,8,128]{2,1,0:T(8,128)S(1)}, bf16[2,512,1024]{2,1,0:T(8,128)(2,1)S(1)}) custom-call(bf16[3,128,512]{2,1,0:T(8,128)(2,1)} %bitcast.5, f32[3,7,512]{2,1,0:T(8,128)} %bitcast.7, bf16[32,2048]{1,0:T(8,128)(2,1)} %lf_hbm.1, bf16[512,8192]{1,0:T(8,128)(2,1)} %w_hbm.7), custom_call_target="tpu_custom_call" | custom-call | tf_op jit(solution)/shard_map/pallas_call | solution.py:288
  15.6 8.4 %all-to-all-done.x_ref = bf16[32,24,128]{2,1,0:T(8,128)(2,1)S(1)} async-done(((bf16[32,24,128]{2,1,0:T(8,128)(2,1)}), bf16[32,24,128]{2,1,0:T(8,128)(2,1)S(1)}, u32[]{:S(2)}, u32[]{:S(2)}) %all-to-all-start) | async-done | bytes 196640 | tf_op jit(solution)/shard_map/all_to_all | solution.py:287
  24.0 0.8 %shard_map.48 = bf16[32,16,128]{2,1,0:T(8,128)(2,1)S(1)} custom-call(bf16[32,24,128]{2,1,0:T(8,128)(2,1)S(1)} %all-to-all-done.x_ref, bf16[2176,128]{1,0:T(8,128)(2,1)S(1)} %get-tuple-element.19.t_ref, f32[7,8,128]{2,1,0:T(8,128)S(1)} %get-tuple-element.20.coef_ref), custom_call_target="tpu_custom_call" | custom-call | tf_op jit(solution)/shard_map/pallas_call | solution.py:305
  24.8 14.4 %all_to_all.10 = bf16[32,16,128]{2,1,0:T(8,128)(2,1)S(1)} all-to-all(bf16[32,16,128]{2,1,0:T(8,128)(2,1)S(1)} %shard_map.48), channel_id=1, replica_groups=mesh['ctx'=32,'tp'=8] {'ctx'}, dimensions={0} | all-to-all | bytes 262144 | tf_op jit(solution)/shard_map/all_to_all | solution.py:314
  39.2 0.5 shard_map.49
  39.7 0.1 collective-permute-start
  39.8 1.9 %shard_map.50.own_ref = bf16[2,128,1024]{2,1,0:T(8,128)(2,1)S(1)} custom-call(bf16[128,512]{1,0:T(8,128)(2,1)S(1)} %get-tuple-element.24.ht_ref.ht_in_ref, bf16[512,8192]{1,0:T(8,128)(2,1)} %w_hbm.7), custom_call_target="tpu_custom_call" | custom-call | flops 268435456 | bytes 2097152 | tf_op jit(solution)/shard_map/pallas_call | solution.py:317
  41.7 0.1 shard_map.51
  41.8 0.1 shard_map.52
  41.8 1.9 %shard_map.53 = bf16[2,128,1024]{2,1,0:T(8,128)(2,1)S(1)} custom-call(bf16[128,512]{1,0:T(8,128)(2,1)S(1)} %get-tuple-element.26.ht_ref, bf16[512,8192]{1,0:T(8,128)(2,1)} %w_hbm.7), custom_call_target="tpu_custom_call" | custom-call | flops 268435456 | bytes 2097152 | tf_op jit(solution)/shard_map/pallas_call | solution.py:317
  43.8 0.6 collective-permute-start.1
  44.3 1.6 %collective-permute-start.2 = (bf16[2,128,640]{2,1,0:T(8,128)(2,1)S(1)}, bf16[2,128,640]{2,1,0:T(8,128)(2,1)S(1)}, u32[]{:S(2)}, u32[]{:S(2)}) collective-permute-start(bf16[2,128,640]{2,1,0:T(8,128)(2,1)S(1)} %get-tuple-element.27), channel_id=1, source_target_pairs={{0,2},{1,7},{2,0},{3,5},{4,6},{5,3},{6,4},{7,1},{8,10},{9,15},{10,... | collective-permute-start | bytes 983048 | tf_op jit(solution)/shard_map/ppermute | solution.py:327
  45.9 0.4 collective-permute-start.3
  46.3 1.9 %shard_map.54.own_ref = bf16[2,128,1024]{2,1,0:T(8,128)(2,1)S(1)} custom-call(bf16[128,512]{1,0:T(8,128)(2,1)S(1)} %get-tuple-element.26.ht_ref, bf16[512,8192]{1,0:T(8,128)(2,1)} %w_hbm.7), custom_call_target="tpu_custom_call" | custom-call | flops 268435456 | bytes 2097152 | tf_op jit(solution)/shard_map/pallas_call | solution.py:317
  48.2 3.2 %collective-permute-done.2.in_ref = bf16[2,128,640]{2,1,0:T(8,128)(2,1)S(1)} collective-permute-done((bf16[2,128,640]{2,1,0:T(8,128)(2,1)S(1)}, bf16[2,128,640]{2,1,0:T(8,128)(2,1)S(1)}, u32[]{:S(2)}, u32[]{:S(2)}) %collective-permute-start.2) | collective-permute-done | bytes 327712 | tf_op jit(solution)/shard_map/ppermute | solution.py:327
  51.4 0.1 shard_map.55
  51.5 3.1 %collective-permute-start.4 = (bf16[128,640]{1,0:T(8,128)(2,1)S(1)}, bf16[128,640]{1,0:T(8,128)(2,1)S(1)}, u32[]{:S(2)}, u32[]{:S(2)}) collective-permute-start(bf16[128,640]{1,0:T(8,128)(2,1)S(1)} %get-tuple-element.31), channel_id=1, source_target_pairs={{0,6},{1,3},{2,4},{3,1},{4,2},{5,7},{6,0},{7,5},{8,14},{9,11},{10,... | collective-permute-start | bytes 491528 | tf_op jit(solution)/shard_map/ppermute | solution.py:327
  54.6 0.1 shard_map.56
  54.7 2.0 %collective-permute-start.5 = (bf16[128,384]{1,0:T(8,128)(2,1)S(1)}, bf16[128,384]{1,0:T(8,128)(2,1)S(1)}, u32[]{:S(2)}, u32[]{:S(2)}) collective-permute-start(bf16[128,384]{1,0:T(8,128)(2,1)S(1)} %get-tuple-element.32), channel_id=1, source_target_pairs={{0,6},{1,3},{2,4},{3,1},{4,2},{5,7},{6,0},{7,5},{8,14},{9,11},{10,... | collective-permute-start | bytes 294920 | tf_op jit(solution)/shard_map/ppermute | solution.py:327
  56.7 3.9 %collective-permute-done.5.refs_3_ = bf16[128,384]{1,0:T(8,128)(2,1)S(1)} collective-permute-done((bf16[128,384]{1,0:T(8,128)(2,1)S(1)}, bf16[128,384]{1,0:T(8,128)(2,1)S(1)}, u32[]{:S(2)}, u32[]{:S(2)}) %collective-permute-start.5) | collective-permute-done | bytes 98336 | tf_op jit(solution)/shard_map/ppermute | solution.py:327
  60.6 0.0 collective-permute-done.4.refs_2_
  60.6 0.8 %shard_map.57 = bf16[128,1024]{1,0:T(8,128)(2,1)} custom-call(f32[128,640]{1,0:T(8,128)S(1)} %get-tuple-element.28.refs_0_, f32[128,384]{1,0:T(8,128)S(1)} %get-tuple-element.30.refs_1_, bf16[128,640]{1,0:T(8,128)(2,1)S(1)} %collective-permute-done.4.refs_2_, bf16[128,384]{1,0:T(8,128)(2,1)S(1)} %collective-permute-done.5.refs_3_), custom_call_target="tpu_custom_call" | custom-call | tf_op jit(solution)/shard_map/pallas_call | solution.py:359
  (3 shorter events, 0.0 us)
Async XLA Ops:
  2.2 21.8 %all-to-all-start = ((bf16[32,24,128]{2,1,0:T(8,128)(2,1)}), bf16[32,24,128]{2,1,0:T(8,128)(2,1)S(1)}, u32[]{:S(2)}, u32[]{:S(2)}) async-start(bf16[32,24,128]{2,1,0:T(8,128)(2,1)} %shard_map.46), calls=%async_computation | async-start | bytes 393216 | tf_op jit(solution)/shard_map/all_to_all | solution.py:287
  39.7 2.0 %collective-permute-start = (bf16[2,128,1024]{2,1,0:T(8,128)(2,1)S(1)}, bf16[2,128,1024]{2,1,0:T(8,128)(2,1)S(1)}, u32[]{:S(2)}, u32[]{:S(2)}) collective-permute-start(bf16[2,128,1024]{2,1,0:T(8,128)(2,1)S(1)} %get-tuple-element.23), channel_id=1, source_target_pairs={{0,1},{1,0},{2,3},{3,2},{4,5},{5,4},{6,7},{7,6},{8,9},{9,8},{10,11... | collective-permute-start | bytes 1572872 | tf_op jit(solution)/shard_map/ppermute | solution.py:327
  43.8 7.6 %collective-permute-start.1 = (bf16[2,128,1024]{2,1,0:T(8,128)(2,1)S(1)}, bf16[2,128,1024]{2,1,0:T(8,128)(2,1)S(1)}, u32[]{:S(2)}, u32[]{:S(2)}) collective-permute-start(bf16[2,128,1024]{2,1,0:T(8,128)(2,1)S(1)} %shard_map.53), channel_id=1, source_target_pairs={{0,1},{1,0},{2,3},{3,2},{4,5},{5,4},{6,7},{7,6},{8,9},{9,8},{10,11... | collective-permute-start | bytes 1572872 | tf_op jit(solution)/shard_map/ppermute | solution.py:327
  44.3 7.1 %collective-permute-start.2 = (bf16[2,128,640]{2,1,0:T(8,128)(2,1)S(1)}, bf16[2,128,640]{2,1,0:T(8,128)(2,1)S(1)}, u32[]{:S(2)}, u32[]{:S(2)}) collective-permute-start(bf16[2,128,640]{2,1,0:T(8,128)(2,1)S(1)} %get-tuple-element.27), channel_id=1, source_target_pairs={{0,2},{1,7},{2,0},{3,5},{4,6},{5,3},{6,4},{7,1},{8,10},{9,15},{10,... | collective-permute-start | bytes 983048 | tf_op jit(solution)/shard_map/ppermute | solution.py:327
  45.9 8.7 %collective-permute-start.3 = (bf16[2,128,384]{2,1,0:T(8,128)(2,1)S(1)}, bf16[2,128,384]{2,1,0:T(8,128)(2,1)S(1)}, u32[]{:S(2)}, u32[]{:S(2)}) collective-permute-start(bf16[2,128,384]{2,1,0:T(8,128)(2,1)S(1)} %get-tuple-element.29), channel_id=1, source_target_pairs={{0,2},{1,7},{2,0},{3,5},{4,6},{5,3},{6,4},{7,1},{8,10},{9,15},{10,... | collective-permute-start | bytes 589832 | tf_op jit(solution)/shard_map/ppermute | solution.py:327
  51.5 9.1 %collective-permute-start.4 = (bf16[128,640]{1,0:T(8,128)(2,1)S(1)}, bf16[128,640]{1,0:T(8,128)(2,1)S(1)}, u32[]{:S(2)}, u32[]{:S(2)}) collective-permute-start(bf16[128,640]{1,0:T(8,128)(2,1)S(1)} %get-tuple-element.31), channel_id=1, source_target_pairs={{0,6},{1,3},{2,4},{3,1},{4,2},{5,7},{6,0},{7,5},{8,14},{9,11},{10,... | collective-permute-start | bytes 491528 | tf_op jit(solution)/shard_map/ppermute | solution.py:327
  54.7 5.9 %collective-permute-start.5 = (bf16[128,384]{1,0:T(8,128)(2,1)S(1)}, bf16[128,384]{1,0:T(8,128)(2,1)S(1)}, u32[]{:S(2)}, u32[]{:S(2)}) collective-permute-start(bf16[128,384]{1,0:T(8,128)(2,1)S(1)} %get-tuple-element.32), channel_id=1, source_target_pairs={{0,6},{1,3},{2,4},{3,1},{4,2},{5,7},{6,0},{7,5},{8,14},{9,11},{10,... | collective-permute-start | bytes 294920 | tf_op jit(solution)/shard_map/ppermute | solution.py:327

commit v5 on v4

--- a/solution.py
+++ b/solution.py
@@ -13,8 +13,6 @@
 HBM = pl.BlockSpec(memory_space=pltpu.HBM)
 
 EDGE = 8
-SPLIT = (0, 640, 1024)
-CHUNKS = len(SPLIT) - 1
 
 
 def in_hbm(x):
@@ -223,36 +221,41 @@
     mixed = h_ref[...].T
     ht_ref[...] = (gate_ref[...] * mixed.astype(F32)).astype(BF)
     ht_ref[:EDGE, :] = mixed[:EDGE]
-    for slot in range(2):
-        out_ref[slot] = product(ht_ref[...], w_ref[slot])
-
-
-def fetched_kernel(ht_ref, w_hbm, out_ref, w_ref, sems, *, first, own):
-    copies = fetches(w_hbm, w_ref, sems, blocks_of(first, own))
-    for slot in range(2):
-        copies[slot].wait()
-        out_ref[slot] = product(ht_ref[...], w_ref[slot])
-
-
-def join_kernel(got_ref, own_ref, ht_in_ref, out_ref, ht_ref, *, chunk):
+    out_ref[...] = product(ht_ref[...], w_ref[1])
+
+
+def first_own_kernel(ht_ref, theirs_ref, w_hbm, own_ref, out_ref, w_ref, sems):
+    copies = fetches(w_hbm, w_ref, sems, blocks_of(True, True)[1:])
+    out_ref[...] = product(ht_ref[...], theirs_ref[0])
+    copies[0].wait()
+    own_ref[...] = product(ht_ref[...], w_ref[0])
+
+
+def fetched_kernel(ht_ref, w_hbm, *refs, wanted):
+    *out_refs, w_ref, sems = refs
+    copies = fetches(w_hbm, w_ref, sems, [blocks_of(first, own)[slot] for first, own, slot in wanted])
+    for copy, out_ref, slot in zip(copies, out_refs, range(len(wanted))):
+        copy.wait()
+        out_ref[...] = product(ht_ref[...], w_ref[slot])
+
+
+def join_kernel(got_ref, own_ref, ht_in_ref, out_ref, ht_ref):
     ht_ref[...] = ht_in_ref[...]
-    lanes = slice(SPLIT[chunk], SPLIT[chunk + 1])
-    out_ref[...] = (got_ref[:, :, lanes].astype(F32) + own_ref[:, :, lanes].astype(F32)).astype(BF)
-
-
-def pass_kernel(got_ref, own_ref, in_ref, *refs, chunk):
-    out_ref, kept_ref = refs[-2:]
-    lanes = slice(SPLIT[chunk], SPLIT[chunk + 1])
-    total = got_ref[:, :, lanes].astype(F32) + own_ref[:, :, lanes].astype(F32) + in_ref[...].astype(F32)
-    kept_ref[...] = total[0]
-    out_ref[...] = total[1].astype(BF)
-
-
-def finish_kernel(*refs):
-    *in_refs, out_ref = refs
-    for i in range(CHUNKS):
-        total = in_refs[i][...] + in_refs[CHUNKS + i][...].astype(F32)
-        out_ref[:, SPLIT[i] : SPLIT[i + 1]] = total.astype(BF)
+    out_ref[...] = (got_ref[...].astype(F32) + own_ref[...].astype(F32)).astype(BF)
+
+
+def pass_kernel(got_ref, own_ref, in_ref, ht_in_ref, out_ref, ht_ref):
+    ht_ref[...] = ht_in_ref[...]
+    total = got_ref[...].astype(F32) + own_ref[...].astype(F32) + in_ref[...].astype(F32)
+    out_ref[...] = total.astype(BF)
+
+
+def keep_kernel(got_ref, own_ref, in_ref, kept_ref):
+    kept_ref[...] = got_ref[...].astype(F32) + own_ref[...].astype(F32) + in_ref[...].astype(F32)
+
+
+def finish_kernel(kept_ref, in_ref, out_ref):
+    out_ref[...] = (kept_ref[...] + in_ref[...].astype(F32)).astype(BF)
 
 
 def body(projected, short_filter, long_filter, out_weight):
@@ -313,14 +316,15 @@
     )(spread, toeplitz, coef)
     mixed = lax.all_to_all(mixed, "ctx", 0, 0, tiled=True).reshape(channels, tok)
 
-    def project(ht, first, own):
+    def project(ht, wanted):
+        count = len(wanted)
         return call(
-            functools.partial(fetched_kernel, first=first, own=own),
-            shaped((2, tok, cols)),
+            functools.partial(fetched_kernel, wanted=wanted),
+            [shaped((tok, cols))] * count,
             [VMEM, HBM],
-            scratch=(pltpu.VMEM((2, channels, cols), BF), pltpu.SemaphoreType.DMA((2,))),
-            flops=4 * tok * channels * cols,
-            nbytes=4 * channels * cols,
+            scratch=(pltpu.VMEM((count, channels, cols), BF), pltpu.SemaphoreType.DMA((count,))),
+            flops=2 * count * tok * channels * cols,
+            nbytes=2 * count * channels * cols,
         )(ht, weight)
 
     def swap(x, peer):
@@ -332,31 +336,35 @@
     def hop(i, parity):
         return i ^ 2 if (i + parity) % 2 == 0 else (3 - i // 2) * 2 + i % 2
 
-    widths = [SPLIT[i + 1] - SPLIT[i] for i in range(CHUNKS)]
-    theirs, ht = call(
-        first_theirs_kernel, [shaped((2, tok, cols)), shaped((tok, channels))], [VMEM] * 3
-    )(mixed, gate, theirs_weight)
+    block = shaped((tok, cols))
+    rows = shaped((tok, channels))
+    near_hop = functools.partial(hop, parity=0)
+    far_hop = functools.partial(hop, parity=1)
+
+    theirs, ht = call(first_theirs_kernel, [block, rows], [VMEM] * 3)(mixed, gate, theirs_weight)
     got = swap(theirs, partner)
-    own = project(ht, True, True)
-    arrived = []
-    for i in range(CHUNKS):
-        send, ht = call(
-            functools.partial(join_kernel, chunk=i), [shaped((2, tok, widths[i])), shaped((tok, channels))], [VMEM] * 3
-        )(got, own, ht)
-        arrived.append(swap(send, functools.partial(hop, parity=0)))
-    theirs = project(ht, False, False)
+    own, theirs = call(
+        first_own_kernel,
+        [block] * 2,
+        [VMEM] * 2 + [HBM],
+        scratch=(pltpu.VMEM((1, channels, cols), BF), pltpu.SemaphoreType.DMA((1,))),
+    )(ht, theirs_weight, weight)
+    send, ht = call(join_kernel, [block, rows], [VMEM] * 3)(got, own, ht)
+    onward = swap(send, near_hop)
+
     got = swap(theirs, partner)
-    own = project(ht, False, True)
-    kept, last = [], []
-    for i in range(CHUNKS):
-        onward, keep = call(
-            functools.partial(pass_kernel, chunk=i),
-            [shaped((tok, widths[i])), shaped((tok, widths[i]), F32)],
-            [VMEM] * (3 + min(i, 1)),
-        )(got, own, arrived[i], *kept[-1:])
-        kept.append(keep)
-        last.append(swap(onward, functools.partial(hop, parity=1)))
-    return call(finish_kernel, shaped((tok, cols)), [VMEM] * (2 * CHUNKS))(*kept, *last)
+    own, theirs = project(ht, ((True, True, 0), (False, False, 1)))
+    send, ht = call(join_kernel, [block, rows], [VMEM] * 3)(got, own, ht)
+    stayed = swap(send, near_hop)
+    got = swap(theirs, partner)
+    (own,) = project(ht, ((False, True, 1),))
+    send, ht = call(pass_kernel, [block, rows], [VMEM] * 4)(got, own, onward, ht)
+    last = swap(send, far_hop)
+
+    theirs, own = project(ht, ((False, False, 0), (False, True, 0)))
+    got = swap(theirs, partner)
+    kept = call(keep_kernel, shaped((tok, cols), F32), [VMEM] * 3)(got, own, stayed)
+    return call(finish_kernel, block, [VMEM] * 2)(kept, last)
 
 
 def solution(mesh):

time: 61.8 us -> 60.7 us (0.982)
  waiting for transfers between devices: 15.5 us -> 14.1 us
  Pallas kernels: 12 us -> 13.2 us
  starting transfers between devices: 19.4 us -> 18.4 us
    ppermute x6 -> x7, waiting for transfers between devices: 7.11 us -> 5.72 us  [swap(): return lax.ppermute(x, 'tp', [(i, peer(i)) for i in range(n_tp)])]
    pallas_call x9 -> x10, Pallas kernels: 7.22 us -> 8.45 us  [the longest x3 5.32 us: project(): call(functools.partial(fetched_kernel, wanted=wanted), [shaped((tok, cols...]
    ppermute x6 -> x7, starting transfers between devices: 7.76 us -> 6.78 us  [swap(): return lax.ppermute(x, 'tp', [(i, peer(i)) for i in range(n_tp)])]
  transfers between devices with their start and end apart: 7 -> 8, of which waited for: 3 -> 2; matrix products, arithmetic and copies ran while one was open for 0% -> 0% of each run, Pallas kernels for 9% -> 15%
where the time goes in v5:
time: 60.7 us; the launch traced here: 60.2 us
  starting transfers between devices  18.4 us (30%)
  blocking collectives  14.4 us (24%)
  waiting for transfers between devices  14.1 us (23%)
  Pallas kernels  13.2 us (22%)
    all_to_all x1, blocking collectives, body(): lax.all_to_all(mixed, 'ctx', 0, 0, tiled=True).reshape(channels, tok)  14.4 us
    all_to_all x1, starting transfers between devices, body(): spread = lax.all_to_all(packed, 'ctx', 0, 0, tiled=True)  11.6 us
    all_to_all x1, waiting for transfers between devices, body(): spread = lax.all_to_all(packed, 'ctx', 0, 0, tiled=True)  8.37 us
    ppermute x7, starting transfers between devices, swap(): return lax.ppermute(x, 'tp', [(i, peer(i)) for i in range(n_tp)])  6.78 us
    ppermute x7, waiting for transfers between devices, swap(): return lax.ppermute(x, 'tp', [(i, peer(i)) for i in range(n_tp)])  5.72 us
    pallas_call x3, Pallas kernels, project(): call(functools.partial(fetched_kernel, wanted=wanted), [shaped((tok, cols...  5.32 us
    pallas_call x1, Pallas kernels, body(): call(functools.partial(pack_kernel, gsize=gsize), shaped((groups, gsize +...  2.21 us
    pallas_call x1, Pallas kernels, body(): call(functools.partial(prep_kernel, gsize=gsize), [shaped((lags * tok, to...  1.76 us
  transfers between devices with their start and end apart: 8, of which 2 were waited for; matrix products, arithmetic and copies ran while one was open for 0% of the time, Pallas kernels for 15%

profile of v5, /device:TPU:2, one launch (start us, length us, event | category | flops | bytes accessed | tf_op | source)
XLA Modules:
  0.0 60.2 jit_solution(1549828382679948035)
XLA Ops:
  0.0 2.2 %shard_map.46 = bf16[32,24,128]{2,1,0:T(8,128)(2,1)} custom-call(bf16[3,128,512]{2,1,0:T(8,128)(2,1)} %bitcast.4, f32[3,7,512]{2,1,0:T(8,128)} %bitcast.6), custom_call_target="tpu_custom_call" | custom-call | tf_op jit(solution)/shard_map/pallas_call | solution.py:275
  2.2 11.6 %all-to-all-start = ((bf16[32,24,128]{2,1,0:T(8,128)(2,1)}), bf16[32,24,128]{2,1,0:T(8,128)(2,1)S(1)}, u32[]{:S(2)}, u32[]{:S(2)}) async-start(bf16[32,24,128]{2,1,0:T(8,128)(2,1)} %shard_map.46), calls=%async_computation | async-start | bytes 393216 | tf_op jit(solution)/shard_map/all_to_all | solution.py:290
  13.9 1.8 %shard_map.47 = (bf16[2176,128]{1,0:T(8,128)(2,1)S(1)}, f32[128,512]{1,0:T(8,128)S(1)}, f32[7,8,128]{2,1,0:T(8,128)S(1)}, bf16[2,512,1024]{2,1,0:T(8,128)(2,1)S(1)}) custom-call(bf16[3,128,512]{2,1,0:T(8,128)(2,1)} %bitcast.5, f32[3,7,512]{2,1,0:T(8,128)} %bitcast.7, bf16[32,2048]{1,0:T(8,128)(2,1)} %lf_hbm.1, bf16[512,8192]{1,0:T(8,128)(2,1)} %w_hbm.9), custom_call_target="tpu_custom_call" | custom-call | tf_op jit(solution)/shard_map/pallas_call | solution.py:291
  15.6 8.4 %all-to-all-done.x_ref = bf16[32,24,128]{2,1,0:T(8,128)(2,1)S(1)} async-done(((bf16[32,24,128]{2,1,0:T(8,128)(2,1)}), bf16[32,24,128]{2,1,0:T(8,128)(2,1)S(1)}, u32[]{:S(2)}, u32[]{:S(2)}) %all-to-all-start) | async-done | bytes 196640 | tf_op jit(solution)/shard_map/all_to_all | solution.py:290
  24.0 0.8 %shard_map.48 = bf16[32,16,128]{2,1,0:T(8,128)(2,1)S(1)} custom-call(bf16[32,24,128]{2,1,0:T(8,128)(2,1)S(1)} %all-to-all-done.x_ref, bf16[2176,128]{1,0:T(8,128)(2,1)S(1)} %get-tuple-element.23.t_ref, f32[7,8,128]{2,1,0:T(8,128)S(1)} %get-tuple-element.24.coef_ref), custom_call_target="tpu_custom_call" | custom-call | tf_op jit(solution)/shard_map/pallas_call | solution.py:308
  24.8 14.4 %all_to_all.10 = bf16[32,16,128]{2,1,0:T(8,128)(2,1)S(1)} all-to-all(bf16[32,16,128]{2,1,0:T(8,128)(2,1)S(1)} %shard_map.48), channel_id=1, replica_groups=mesh['ctx'=32,'tp'=8] {'ctx'}, dimensions={0} | all-to-all | bytes 262144 | tf_op jit(solution)/shard_map/all_to_all | solution.py:317
  39.2 0.3 shard_map.49
  39.5 0.1 collective-permute-start
  39.6 1.7 %shard_map.50 = (bf16[128,1024]{1,0:T(8,128)(2,1)S(1)}, bf16[128,1024]{1,0:T(8,128)(2,1)S(1)}) custom-call(bf16[128,512]{1,0:T(8,128)(2,1)S(1)} %get-tuple-element.28.ht_ref.ht_in_ref, bf16[2,512,1024]{2,1,0:T(8,128)(2,1)S(1)} %get-tuple-element.26.w_ref.theirs_ref, bf16[512,8192]{1,0:T(8,128)(2,1)} %w_hbm.9), custom_call_target="tpu_custom_call" | custom-call | tf_op jit(solution)/shard_map/pallas_call | solution.py:346
  41.4 0.6 collective-permute-start.2
  41.9 0.1 shard_map.51
  42.0 1.7 %collective-permute-start.3 = (bf16[128,1024]{1,0:T(8,128)(2,1)S(1)}, bf16[128,1024]{1,0:T(8,128)(2,1)S(1)}, u32[]{:S(2)}, u32[]{:S(2)}) collective-permute-start(bf16[128,1024]{1,0:T(8,128)(2,1)S(1)} %get-tuple-element.35), channel_id=1, source_target_pairs={{0,2},{1,7},{2,0},{3,5},{4,6},{5,3},{6,4},{7,1},{8,10},{9,15},{10,... | collective-permute-start | bytes 786440 | tf_op jit(solution)/shard_map/ppermute | solution.py:331
  43.7 1.9 %shard_map.52 = (bf16[128,1024]{1,0:T(8,128)(2,1)S(1)}, bf16[128,1024]{1,0:T(8,128)(2,1)S(1)}) custom-call(bf16[128,512]{1,0:T(8,128)(2,1)S(1)} %get-tuple-element.30.ht_ref.ht_in_ref, bf16[512,8192]{1,0:T(8,128)(2,1)} %w_hbm.9), custom_call_target="tpu_custom_call" | custom-call | flops 268435456 | bytes 2097152 | tf_op jit(solution)/shard_map/pallas_call | solution.py:321
  45.6 1.3 %collective-permute-start.1 = (bf16[128,1024]{1,0:T(8,128)(2,1)S(1)}, bf16[128,1024]{1,0:T(8,128)(2,1)S(1)}, u32[]{:S(2)}, u32[]{:S(2)}) collective-permute-start(bf16[128,1024]{1,0:T(8,128)(2,1)S(1)} %get-tuple-element.31), channel_id=1, source_target_pairs={{0,1},{1,0},{2,3},{3,2},{4,5},{5,4},{6,7},{7,6},{8,9},{9,8},{10,11... | collective-permute-start | bytes 786440 | tf_op jit(solution)/shard_map/ppermute | solution.py:331
  46.8 0.1 shard_map.53
  46.9 0.2 collective-permute-start.5
  47.1 1.6 %shard_map.54.own_ref = bf16[128,1024]{1,0:T(8,128)(2,1)S(1)} custom-call(bf16[128,512]{1,0:T(8,128)(2,1)S(1)} %get-tuple-element.34.ht_ref.ht_in_ref, bf16[512,8192]{1,0:T(8,128)(2,1)} %w_hbm.9), custom_call_target="tpu_custom_call" | custom-call | flops 134217728 | bytes 1048576 | tf_op jit(solution)/shard_map/pallas_call | solution.py:321
  48.7 0.1 shard_map.55
  48.8 1.9 %shard_map.56 = (bf16[128,1024]{1,0:T(8,128)(2,1)S(1)}, bf16[128,1024]{1,0:T(8,128)(2,1)S(1)}) custom-call(bf16[128,512]{1,0:T(8,128)(2,1)S(1)} %get-tuple-element.36.ht_ref, bf16[512,8192]{1,0:T(8,128)(2,1)} %w_hbm.9), custom_call_target="tpu_custom_call" | custom-call | flops 268435456 | bytes 2097152 | tf_op jit(solution)/shard_map/pallas_call | solution.py:321
  50.7 1.2 %collective-permute-start.4 = (bf16[128,1024]{1,0:T(8,128)(2,1)S(1)}, bf16[128,1024]{1,0:T(8,128)(2,1)S(1)}, u32[]{:S(2)}, u32[]{:S(2)}) collective-permute-start(bf16[128,1024]{1,0:T(8,128)(2,1)S(1)} %get-tuple-element.37), channel_id=1, source_target_pairs={{0,1},{1,0},{2,3},{3,2},{4,5},{5,4},{6,7},{7,6},{8,9},{9,8},{10,11... | collective-permute-start | bytes 786440 | tf_op jit(solution)/shard_map/ppermute | solution.py:331
  51.9 1.8 %collective-permute-start.6 = (bf16[128,1024]{1,0:T(8,128)(2,1)S(1)}, bf16[128,1024]{1,0:T(8,128)(2,1)S(1)}, u32[]{:S(2)}, u32[]{:S(2)}) collective-permute-start(bf16[128,1024]{1,0:T(8,128)(2,1)S(1)} %get-tuple-element.40), channel_id=1, source_target_pairs={{0,6},{1,3},{2,4},{3,1},{4,2},{5,7},{6,0},{7,5},{8,14},{9,11},{10,... | collective-permute-start | bytes 786440 | tf_op jit(solution)/shard_map/ppermute | solution.py:331
  53.7 0.1 shard_map.57.kept_ref
  53.8 5.7 %collective-permute-done.6.in_ref = bf16[128,1024]{1,0:T(8,128)(2,1)S(1)} collective-permute-done((bf16[128,1024]{1,0:T(8,128)(2,1)S(1)}, bf16[128,1024]{1,0:T(8,128)(2,1)S(1)}, u32[]{:S(2)}, u32[]{:S(2)}) %collective-permute-start.6) | collective-permute-done | bytes 262176 | tf_op jit(solution)/shard_map/ppermute | solution.py:331
  59.5 0.7 %shard_map.58 = bf16[128,1024]{1,0:T(8,128)(2,1)} custom-call(f32[128,1024]{1,0:T(8,128)S(1)} %shard_map.57.kept_ref, bf16[128,1024]{1,0:T(8,128)(2,1)S(1)} %collective-permute-done.6.in_ref), custom_call_target="tpu_custom_call" | custom-call | tf_op jit(solution)/shard_map/pallas_call | solution.py:367
  (6 shorter events, 0.0 us)
Async XLA Ops:
  2.2 21.8 %all-to-all-start = ((bf16[32,24,128]{2,1,0:T(8,128)(2,1)}), bf16[32,24,128]{2,1,0:T(8,128)(2,1)S(1)}, u32[]{:S(2)}, u32[]{:S(2)}) async-start(bf16[32,24,128]{2,1,0:T(8,128)(2,1)} %shard_map.46), calls=%async_computation | async-start | bytes 393216 | tf_op jit(solution)/shard_map/all_to_all | solution.py:290
  39.5 2.4 %collective-permute-start = (bf16[128,1024]{1,0:T(8,128)(2,1)S(1)}, bf16[128,1024]{1,0:T(8,128)(2,1)S(1)}, u32[]{:S(2)}, u32[]{:S(2)}) collective-permute-start(bf16[128,1024]{1,0:T(8,128)(2,1)S(1)} %get-tuple-element.27), channel_id=1, source_target_pairs={{0,1},{1,0},{2,3},{3,2},{4,5},{5,4},{6,7},{7,6},{8,9},{9,8},{10,11... | collective-permute-start | bytes 786440 | tf_op jit(solution)/shard_map/ppermute | solution.py:331
  41.4 5.5 %collective-permute-start.2 = (bf16[128,1024]{1,0:T(8,128)(2,1)S(1)}, bf16[128,1024]{1,0:T(8,128)(2,1)S(1)}, u32[]{:S(2)}, u32[]{:S(2)}) collective-permute-start(bf16[128,1024]{1,0:T(8,128)(2,1)S(1)} %get-tuple-element.32), channel_id=1, source_target_pairs={{0,1},{1,0},{2,3},{3,2},{4,5},{5,4},{6,7},{7,6},{8,9},{9,8},{10,11... | collective-permute-start | bytes 786440 | tf_op jit(solution)/shard_map/ppermute | solution.py:331
  42.0 6.7 %collective-permute-start.3 = (bf16[128,1024]{1,0:T(8,128)(2,1)S(1)}, bf16[128,1024]{1,0:T(8,128)(2,1)S(1)}, u32[]{:S(2)}, u32[]{:S(2)}) collective-permute-start(bf16[128,1024]{1,0:T(8,128)(2,1)S(1)} %get-tuple-element.35), channel_id=1, source_target_pairs={{0,2},{1,7},{2,0},{3,5},{4,6},{5,3},{6,4},{7,1},{8,10},{9,15},{10,... | collective-permute-start | bytes 786440 | tf_op jit(solution)/shard_map/ppermute | solution.py:331
  45.6 3.1 %collective-permute-start.1 = (bf16[128,1024]{1,0:T(8,128)(2,1)S(1)}, bf16[128,1024]{1,0:T(8,128)(2,1)S(1)}, u32[]{:S(2)}, u32[]{:S(2)}) collective-permute-start(bf16[128,1024]{1,0:T(8,128)(2,1)S(1)} %get-tuple-element.31), channel_id=1, source_target_pairs={{0,1},{1,0},{2,3},{3,2},{4,5},{5,4},{6,7},{7,6},{8,9},{9,8},{10,11... | collective-permute-start | bytes 786440 | tf_op jit(solution)/shard_map/ppermute | solution.py:331
  46.9 6.8 %collective-permute-start.5 = (bf16[128,1024]{1,0:T(8,128)(2,1)S(1)}, bf16[128,1024]{1,0:T(8,128)(2,1)S(1)}, u32[]{:S(2)}, u32[]{:S(2)}) collective-permute-start(bf16[128,1024]{1,0:T(8,128)(2,1)S(1)} %get-tuple-element.39), channel_id=1, source_target_pairs={{0,2},{1,7},{2,0},{3,5},{4,6},{5,3},{6,4},{7,1},{8,10},{9,15},{10,... | collective-permute-start | bytes 786440 | tf_op jit(solution)/shard_map/ppermute | solution.py:331
  50.7 3.0 %collective-permute-start.4 = (bf16[128,1024]{1,0:T(8,128)(2,1)S(1)}, bf16[128,1024]{1,0:T(8,128)(2,1)S(1)}, u32[]{:S(2)}, u32[]{:S(2)}) collective-permute-start(bf16[128,1024]{1,0:T(8,128)(2,1)S(1)} %get-tuple-element.37), channel_id=1, source_target_pairs={{0,1},{1,0},{2,3},{3,2},{4,5},{5,4},{6,7},{7,6},{8,9},{9,8},{10,11... | collective-permute-start | bytes 786440 | tf_op jit(solution)/shard_map/ppermute | solution.py:331
  51.9 7.6 %collective-permute-start.6 = (bf16[128,1024]{1,0:T(8,128)(2,1)S(1)}, bf16[128,1024]{1,0:T(8,128)(2,1)S(1)}, u32[]{:S(2)}, u32[]{:S(2)}) collective-permute-start(bf16[128,1024]{1,0:T(8,128)(2,1)S(1)} %get-tuple-element.40), channel_id=1, source_target_pairs={{0,6},{1,3},{2,4},{3,1},{4,2},{5,7},{6,0},{7,5},{8,14},{9,11},{10,... | collective-permute-start | bytes 786440 | tf_op jit(solution)/shard_map/ppermute | solution.py:331

commit v6 on v5

--- a/solution.py
+++ b/solution.py
@@ -13,6 +13,7 @@
 HBM = pl.BlockSpec(memory_space=pltpu.HBM)
 
 EDGE = 8
+EARLY = 384
 
 
 def in_hbm(x):
@@ -126,7 +127,7 @@
 
 
 def prep_kernel(
-    x_hbm, sf_hbm, lf_hbm, w_hbm, g_ref, gate_ref, coef_ref, w_ref, x_ref, sf_ref, lf_ref, sems, w_sems, *, gsize
+    x_hbm, sf_hbm, lf_hbm, w_hbm, g_ref, gate_ref, coef_ref, w_ref, early_ref, x_ref, sf_ref, lf_ref, sems, w_sems, *, gsize
 ):
     tok, channels = x_ref.shape
     _, taps, _ = sf_ref.shape
@@ -140,6 +141,9 @@
     for copy in copies:
         copy.start()
     fetched = fetches(w_hbm, w_ref, w_sems, blocks_of(True, False))
+    start = pl.multiple_of(blocks_of(True, True)[1] * w_ref.shape[2], 128)
+    fetched.append(pltpu.make_async_copy(w_hbm.at[:, pl.ds(start, EARLY)], early_ref, w_sems.at[2]))
+    fetched[2].start()
     me = lax.axis_index("ctx")
     for copy in copies:
         copy.wait()
@@ -224,11 +228,15 @@
     out_ref[...] = product(ht_ref[...], w_ref[1])
 
 
-def first_own_kernel(ht_ref, theirs_ref, w_hbm, own_ref, out_ref, w_ref, sems):
-    copies = fetches(w_hbm, w_ref, sems, blocks_of(True, True)[1:])
+def first_own_kernel(ht_ref, theirs_ref, early_ref, w_hbm, own_ref, out_ref, w_ref, sem):
+    rest = w_ref.shape[1]
+    start = pl.multiple_of(blocks_of(True, True)[1] * (EARLY + rest) + EARLY, 128)
+    copy = pltpu.make_async_copy(w_hbm.at[:, pl.ds(start, rest)], w_ref, sem)
+    copy.start()
     out_ref[...] = product(ht_ref[...], theirs_ref[0])
-    copies[0].wait()
-    own_ref[...] = product(ht_ref[...], w_ref[0])
+    own_ref[:, :EARLY] = product(ht_ref[...], early_ref[...])
+    copy.wait()
+    own_ref[:, EARLY:] = product(ht_ref[...], w_ref[...])
 
 
 def fetched_kernel(ht_ref, w_hbm, *refs, wanted):
@@ -288,13 +296,14 @@
         out_specs=HBM,
     )(x, sf)
     spread = lax.all_to_all(packed, "ctx", 0, 0, tiled=True)
-    toeplitz, gate, coef, theirs_weight = call(
+    toeplitz, gate, coef, theirs_weight, early = call(
         functools.partial(prep_kernel, gsize=gsize),
         [
             shaped((lags * tok, tok)),
             shaped((tok, channels), F32),
             shaped((taps, 8, 128), F32),
             shaped((2, channels, cols)),
+            shaped((channels, EARLY)),
         ],
         [HBM] * 4,
         scratch=(
@@ -302,7 +311,7 @@
             pltpu.VMEM((feats, taps, channels), F32),
             pltpu.VMEM(long_filter.shape, BF),
             pltpu.SemaphoreType.DMA((3,)),
-            pltpu.SemaphoreType.DMA((2,)),
+            pltpu.SemaphoreType.DMA((3,)),
         ),
     )(x, sf, in_hbm(long_filter), weight)
     mixed = call(
@@ -346,9 +355,9 @@
     own, theirs = call(
         first_own_kernel,
         [block] * 2,
-        [VMEM] * 2 + [HBM],
-        scratch=(pltpu.VMEM((1, channels, cols), BF), pltpu.SemaphoreType.DMA((1,))),
-    )(ht, theirs_weight, weight)
+        [VMEM] * 3 + [HBM],
+        scratch=(pltpu.VMEM((channels, cols - EARLY), BF), pltpu.SemaphoreType.DMA),
+    )(ht, theirs_weight, early, weight)
     send, ht = call(join_kernel, [block, rows], [VMEM] * 3)(got, own, ht)
     onward = swap(send, near_hop)
 

time: 60.7 us -> 60.7 us (level)
  transfers between devices with their start and end apart: 8 -> 8, of which waited for: 2 -> 2; matrix products, arithmetic and copies ran while one was open for 0% -> 0% of each run, Pallas kernels for 15% -> 16%
where the time goes in v6:
time: 60.7 us; the launch traced here: 60.2 us
  starting transfers between devices  18.4 us (30%)
  blocking collectives  14.4 us (24%)
  waiting for transfers between devices  13.7 us (23%)
  Pallas kernels  13.6 us (22%)
    all_to_all x1, blocking collectives, body(): lax.all_to_all(mixed, 'ctx', 0, 0, tiled=True).reshape(channels, tok)  14.4 us
    all_to_all x1, starting transfers between devices, body(): spread = lax.all_to_all(packed, 'ctx', 0, 0, tiled=True)  11.6 us
    all_to_all x1, waiting for transfers between devices, body(): spread = lax.all_to_all(packed, 'ctx', 0, 0, tiled=True)  7.96 us
    ppermute x7, starting transfers between devices, swap(): return lax.ppermute(x, 'tp', [(i, peer(i)) for i in range(n_tp)])  6.78 us
    ppermute x7, waiting for transfers between devices, swap(): return lax.ppermute(x, 'tp', [(i, peer(i)) for i in range(n_tp)])  5.72 us
    pallas_call x3, Pallas kernels, project(): call(functools.partial(fetched_kernel, wanted=wanted), [shaped((tok, cols...  5.32 us
    pallas_call x1, Pallas kernels, body(): call(functools.partial(pack_kernel, gsize=gsize), shaped((groups, gsize +...  2.21 us
    pallas_call x1, Pallas kernels, body(): call(functools.partial(prep_kernel, gsize=gsize), [shaped((lags * tok, to...  2.17 us
  transfers between devices with their start and end apart: 8, of which 2 were waited for; matrix products, arithmetic and copies ran while one was open for 0% of the time, Pallas kernels for 16%

profile of v6, /device:TPU:2, one launch (start us, length us, event | category | flops | bytes accessed | tf_op | source)
XLA Modules:
  0.0 60.2 jit_solution(2983136944585917981)
XLA Ops:
  0.0 2.2 %shard_map.46 = bf16[32,24,128]{2,1,0:T(8,128)(2,1)} custom-call(bf16[3,128,512]{2,1,0:T(8,128)(2,1)} %bitcast.4, f32[3,7,512]{2,1,0:T(8,128)} %bitcast.6), custom_call_target="tpu_custom_call" | custom-call | tf_op jit(solution)/shard_map/pallas_call | solution.py:283
  2.2 11.6 %all-to-all-start = ((bf16[32,24,128]{2,1,0:T(8,128)(2,1)}), bf16[32,24,128]{2,1,0:T(8,128)(2,1)S(1)}, u32[]{:S(2)}, u32[]{:S(2)}) async-start(bf16[32,24,128]{2,1,0:T(8,128)(2,1)} %shard_map.46), calls=%async_computation | async-start | bytes 393216 | tf_op jit(solution)/shard_map/all_to_all | solution.py:298
  13.9 2.2 %shard_map.47 = (bf16[2176,128]{1,0:T(8,128)(2,1)S(1)}, f32[128,512]{1,0:T(8,128)S(1)}, f32[7,8,128]{2,1,0:T(8,128)S(1)}, bf16[2,512,1024]{2,1,0:T(8,128)(2,1)S(1)}, bf16[512,384]{1,0:T(8,128)(2,1)S(1)}) custom-call(bf16[3,128,512]{2,1,0:T(8,128)(2,1)} %bitcast.5, f32[3,7,512]{2,1,0:T(8,128)} %bitcast.7, bf16[32,2048]{1,0:T(8,128)(2,1)} %lf_hbm.1, ...), custom_call_target="tpu_custom_call" | custom-call | tf_op jit(solution)/shard_map/pallas_call | solution.py:299
  16.0 8.0 %all-to-all-done.x_ref = bf16[32,24,128]{2,1,0:T(8,128)(2,1)S(1)} async-done(((bf16[32,24,128]{2,1,0:T(8,128)(2,1)}), bf16[32,24,128]{2,1,0:T(8,128)(2,1)S(1)}, u32[]{:S(2)}, u32[]{:S(2)}) %all-to-all-start) | async-done | bytes 196640 | tf_op jit(solution)/shard_map/all_to_all | solution.py:298
  24.0 0.8 %shard_map.48 = bf16[32,16,128]{2,1,0:T(8,128)(2,1)S(1)} custom-call(bf16[32,24,128]{2,1,0:T(8,128)(2,1)S(1)} %all-to-all-done.x_ref, bf16[2176,128]{1,0:T(8,128)(2,1)S(1)} %get-tuple-element.24.t_ref, f32[7,8,128]{2,1,0:T(8,128)S(1)} %get-tuple-element.25.coef_ref), custom_call_target="tpu_custom_call" | custom-call | tf_op jit(solution)/shard_map/pallas_call | solution.py:317
  24.8 14.4 %all_to_all.10 = bf16[32,16,128]{2,1,0:T(8,128)(2,1)S(1)} all-to-all(bf16[32,16,128]{2,1,0:T(8,128)(2,1)S(1)} %shard_map.48), channel_id=1, replica_groups=mesh['ctx'=32,'tp'=8] {'ctx'}, dimensions={0} | all-to-all | bytes 262144 | tf_op jit(solution)/shard_map/all_to_all | solution.py:326
  39.2 0.3 shard_map.49
  39.5 0.1 collective-permute-start
  39.6 1.7 %shard_map.50 = (bf16[128,1024]{1,0:T(8,128)(2,1)S(1)}, bf16[128,1024]{1,0:T(8,128)(2,1)S(1)}) custom-call(bf16[128,512]{1,0:T(8,128)(2,1)S(1)} %get-tuple-element.29.ht_ref.ht_in_ref, bf16[2,512,1024]{2,1,0:T(8,128)(2,1)S(1)} %get-tuple-element.27.w_ref.theirs_ref, bf16[512,384]{1,0:T(8,128)(2,1)S(1)} %get-tuple-element.30.early_ref, bf16[512,8192]{1,0:T(8,128)(2,1)} %w_hbm.9), custom_call_target="tpu_custom_call" | custom-call | tf_op jit(solution)/shard_map/pallas_call | solution.py:355
  41.3 0.6 collective-permute-start.2
  41.9 0.1 shard_map.51
  42.0 1.7 %collective-permute-start.3 = (bf16[128,1024]{1,0:T(8,128)(2,1)S(1)}, bf16[128,1024]{1,0:T(8,128)(2,1)S(1)}, u32[]{:S(2)}, u32[]{:S(2)}) collective-permute-start(bf16[128,1024]{1,0:T(8,128)(2,1)S(1)} %get-tuple-element.37), channel_id=1, source_target_pairs={{0,2},{1,7},{2,0},{3,5},{4,6},{5,3},{6,4},{7,1},{8,10},{9,15},{10,... | collective-permute-start | bytes 786440 | tf_op jit(solution)/shard_map/ppermute | solution.py:340
  43.7 1.9 %shard_map.52 = (bf16[128,1024]{1,0:T(8,128)(2,1)S(1)}, bf16[128,1024]{1,0:T(8,128)(2,1)S(1)}) custom-call(bf16[128,512]{1,0:T(8,128)(2,1)S(1)} %get-tuple-element.32.ht_ref.ht_in_ref, bf16[512,8192]{1,0:T(8,128)(2,1)} %w_hbm.9), custom_call_target="tpu_custom_call" | custom-call | flops 268435456 | bytes 2097152 | tf_op jit(solution)/shard_map/pallas_call | solution.py:330
  45.5 1.3 %collective-permute-start.1 = (bf16[128,1024]{1,0:T(8,128)(2,1)S(1)}, bf16[128,1024]{1,0:T(8,128)(2,1)S(1)}, u32[]{:S(2)}, u32[]{:S(2)}) collective-permute-start(bf16[128,1024]{1,0:T(8,128)(2,1)S(1)} %get-tuple-element.33), channel_id=1, source_target_pairs={{0,1},{1,0},{2,3},{3,2},{4,5},{5,4},{6,7},{7,6},{8,9},{9,8},{10,11... | collective-permute-start | bytes 786440 | tf_op jit(solution)/shard_map/ppermute | solution.py:340
  46.8 0.1 shard_map.53
  46.9 0.2 collective-permute-start.5
  47.1 1.6 %shard_map.54.own_ref = bf16[128,1024]{1,0:T(8,128)(2,1)S(1)} custom-call(bf16[128,512]{1,0:T(8,128)(2,1)S(1)} %get-tuple-element.36.ht_ref.ht_in_ref, bf16[512,8192]{1,0:T(8,128)(2,1)} %w_hbm.9), custom_call_target="tpu_custom_call" | custom-call | flops 134217728 | bytes 1048576 | tf_op jit(solution)/shard_map/pallas_call | solution.py:330
  48.7 0.1 shard_map.55
  48.8 1.9 %shard_map.56 = (bf16[128,1024]{1,0:T(8,128)(2,1)S(1)}, bf16[128,1024]{1,0:T(8,128)(2,1)S(1)}) custom-call(bf16[128,512]{1,0:T(8,128)(2,1)S(1)} %get-tuple-element.38.ht_ref, bf16[512,8192]{1,0:T(8,128)(2,1)} %w_hbm.9), custom_call_target="tpu_custom_call" | custom-call | flops 268435456 | bytes 2097152 | tf_op jit(solution)/shard_map/pallas_call | solution.py:330
  50.7 1.2 %collective-permute-start.4 = (bf16[128,1024]{1,0:T(8,128)(2,1)S(1)}, bf16[128,1024]{1,0:T(8,128)(2,1)S(1)}, u32[]{:S(2)}, u32[]{:S(2)}) collective-permute-start(bf16[128,1024]{1,0:T(8,128)(2,1)S(1)} %get-tuple-element.39), channel_id=1, source_target_pairs={{0,1},{1,0},{2,3},{3,2},{4,5},{5,4},{6,7},{7,6},{8,9},{9,8},{10,11... | collective-permute-start | bytes 786440 | tf_op jit(solution)/shard_map/ppermute | solution.py:340
  51.9 1.8 %collective-permute-start.6 = (bf16[128,1024]{1,0:T(8,128)(2,1)S(1)}, bf16[128,1024]{1,0:T(8,128)(2,1)S(1)}, u32[]{:S(2)}, u32[]{:S(2)}) collective-permute-start(bf16[128,1024]{1,0:T(8,128)(2,1)S(1)} %get-tuple-element.42), channel_id=1, source_target_pairs={{0,6},{1,3},{2,4},{3,1},{4,2},{5,7},{6,0},{7,5},{8,14},{9,11},{10,... | collective-permute-start | bytes 786440 | tf_op jit(solution)/shard_map/ppermute | solution.py:340
  53.7 0.1 shard_map.57.kept_ref
  53.8 5.7 %collective-permute-done.6.in_ref = bf16[128,1024]{1,0:T(8,128)(2,1)S(1)} collective-permute-done((bf16[128,1024]{1,0:T(8,128)(2,1)S(1)}, bf16[128,1024]{1,0:T(8,128)(2,1)S(1)}, u32[]{:S(2)}, u32[]{:S(2)}) %collective-permute-start.6) | collective-permute-done | bytes 262176 | tf_op jit(solution)/shard_map/ppermute | solution.py:340
  59.5 0.7 %shard_map.58 = bf16[128,1024]{1,0:T(8,128)(2,1)} custom-call(f32[128,1024]{1,0:T(8,128)S(1)} %shard_map.57.kept_ref, bf16[128,1024]{1,0:T(8,128)(2,1)S(1)} %collective-permute-done.6.in_ref), custom_call_target="tpu_custom_call" | custom-call | tf_op jit(solution)/shard_map/pallas_call | solution.py:376
  (6 shorter events, 0.0 us)
Async XLA Ops:
  2.2 21.8 %all-to-all-start = ((bf16[32,24,128]{2,1,0:T(8,128)(2,1)}), bf16[32,24,128]{2,1,0:T(8,128)(2,1)S(1)}, u32[]{:S(2)}, u32[]{:S(2)}) async-start(bf16[32,24,128]{2,1,0:T(8,128)(2,1)} %shard_map.46), calls=%async_computation | async-start | bytes 393216 | tf_op jit(solution)/shard_map/all_to_all | solution.py:298
  39.5 2.4 %collective-permute-start = (bf16[128,1024]{1,0:T(8,128)(2,1)S(1)}, bf16[128,1024]{1,0:T(8,128)(2,1)S(1)}, u32[]{:S(2)}, u32[]{:S(2)}) collective-permute-start(bf16[128,1024]{1,0:T(8,128)(2,1)S(1)} %get-tuple-element.28), channel_id=1, source_target_pairs={{0,1},{1,0},{2,3},{3,2},{4,5},{5,4},{6,7},{7,6},{8,9},{9,8},{10,11... | collective-permute-start | bytes 786440 | tf_op jit(solution)/shard_map/ppermute | solution.py:340
  41.3 5.5 %collective-permute-start.2 = (bf16[128,1024]{1,0:T(8,128)(2,1)S(1)}, bf16[128,1024]{1,0:T(8,128)(2,1)S(1)}, u32[]{:S(2)}, u32[]{:S(2)}) collective-permute-start(bf16[128,1024]{1,0:T(8,128)(2,1)S(1)} %get-tuple-element.34), channel_id=1, source_target_pairs={{0,1},{1,0},{2,3},{3,2},{4,5},{5,4},{6,7},{7,6},{8,9},{9,8},{10,11... | collective-permute-start | bytes 786440 | tf_op jit(solution)/shard_map/ppermute | solution.py:340
  42.0 6.7 %collective-permute-start.3 = (bf16[128,1024]{1,0:T(8,128)(2,1)S(1)}, bf16[128,1024]{1,0:T(8,128)(2,1)S(1)}, u32[]{:S(2)}, u32[]{:S(2)}) collective-permute-start(bf16[128,1024]{1,0:T(8,128)(2,1)S(1)} %get-tuple-element.37), channel_id=1, source_target_pairs={{0,2},{1,7},{2,0},{3,5},{4,6},{5,3},{6,4},{7,1},{8,10},{9,15},{10,... | collective-permute-start | bytes 786440 | tf_op jit(solution)/shard_map/ppermute | solution.py:340
  45.5 3.1 %collective-permute-start.1 = (bf16[128,1024]{1,0:T(8,128)(2,1)S(1)}, bf16[128,1024]{1,0:T(8,128)(2,1)S(1)}, u32[]{:S(2)}, u32[]{:S(2)}) collective-permute-start(bf16[128,1024]{1,0:T(8,128)(2,1)S(1)} %get-tuple-element.33), channel_id=1, source_target_pairs={{0,1},{1,0},{2,3},{3,2},{4,5},{5,4},{6,7},{7,6},{8,9},{9,8},{10,11... | collective-permute-start | bytes 786440 | tf_op jit(solution)/shard_map/ppermute | solution.py:340
  46.9 6.8 %collective-permute-start.5 = (bf16[128,1024]{1,0:T(8,128)(2,1)S(1)}, bf16[128,1024]{1,0:T(8,128)(2,1)S(1)}, u32[]{:S(2)}, u32[]{:S(2)}) collective-permute-start(bf16[128,1024]{1,0:T(8,128)(2,1)S(1)} %get-tuple-element.41), channel_id=1, source_target_pairs={{0,2},{1,7},{2,0},{3,5},{4,6},{5,3},{6,4},{7,1},{8,10},{9,15},{10,... | collective-permute-start | bytes 786440 | tf_op jit(solution)/shard_map/ppermute | solution.py:340
  50.7 3.0 %collective-permute-start.4 = (bf16[128,1024]{1,0:T(8,128)(2,1)S(1)}, bf16[128,1024]{1,0:T(8,128)(2,1)S(1)}, u32[]{:S(2)}, u32[]{:S(2)}) collective-permute-start(bf16[128,1024]{1,0:T(8,128)(2,1)S(1)} %get-tuple-element.39), channel_id=1, source_target_pairs={{0,1},{1,0},{2,3},{3,2},{4,5},{5,4},{6,7},{7,6},{8,9},{9,8},{10,11... | collective-permute-start | bytes 786440 | tf_op jit(solution)/shard_map/ppermute | solution.py:340
  51.9 7.6 %collective-permute-start.6 = (bf16[128,1024]{1,0:T(8,128)(2,1)S(1)}, bf16[128,1024]{1,0:T(8,128)(2,1)S(1)}, u32[]{:S(2)}, u32[]{:S(2)}) collective-permute-start(bf16[128,1024]{1,0:T(8,128)(2,1)S(1)} %get-tuple-element.42), channel_id=1, source_target_pairs={{0,6},{1,3},{2,4},{3,1},{4,2},{5,7},{6,0},{7,5},{8,14},{9,11},{10,... | collective-permute-start | bytes 786440 | tf_op jit(solution)/shard_map/ppermute | solution.py:340
